TPU v7x, 32 devices: a whole 2x2x4 slice. The times are simulated.
32 devices in a mesh: groups: 2 (over y), tile: 4 (over z), col: 2 (over x), branch: 2 (over core).
Axes of the slice: x: 2, y: 2, z: 4, core: 2. Of those that a mesh axis runs over, the one named last changes fastest.
Arguments:
- alignment_tensor: float32 [4, 64, 256, 256], P(('groups', 'branch'), 'tile', 'col'), parts along dimension 0, may hold values from -6 to 6
- residue_grid: float32 [4, 256, 256, 128], P(('groups', 'branch'), 'tile', 'col'), parts along dimension 0, may hold values from -6 to 6
- mixing_scale_vector: float32 [256], replicated, may hold values from 0.1 to 1.9
- logit_offset_scale: float32 [128], replicated, may hold values from 0.1 to 1.9
- feedforward_scale: float32 [256], replicated, may hold values from 0.1 to 1.9
- product_scale_vector: float32 [256], replicated, may hold values from 0.1 to 1.9
- grid_scale_vector: float32 [128], replicated, may hold values from 0.1 to 1.9
- logit_offset_map: float32 [128, 8], replicated, may hold values from -0.5 to 0.5
- asking_mapping: bfloat16 [256, 256], replicated, may hold values from -0.375 to 0.375
- lookup_mapping: bfloat16 [256, 256], replicated, may hold values from -0.375 to 0.375
- content_mapping: bfloat16 [256, 256], replicated, may hold values from -0.375 to 0.375
- mixing_return_matrix: bfloat16 [256, 256], replicated, may hold values from -0.375 to 0.375
- alignment_widen_map: bfloat16 [256, 1024], replicated, may hold values from -0.375 to 0.375
- alignment_shrink_map: bfloat16 [1024, 256], replicated, may hold values from -0.1875 to 0.1875
- former_embedding_map: bfloat16 [256, 32], replicated, may hold values from -0.375 to 0.375
- latter_embedding_map: bfloat16 [256, 32], replicated, may hold values from -0.375 to 0.375
- product_return_map: float32 [1024, 128], replicated, may hold values from -1 to 1
- grid_widen_map: bfloat16 [128, 512], replicated, may hold values from -0.5 to 0.5
- grid_shrink_map: bfloat16 [512, 128], replicated, may hold values from -0.25 to 0.25
Outputs:
- alignment_revised: float32 [4, 64, 256, 256], P(('groups', 'branch'), 'tile', 'col'), parts along dimension 0
- grid_revised: float32 [4, 256, 256, 128], P(('groups', 'branch'), 'tile', 'col'), parts along dimension 0
There are 2 independent parts, one for each index of `groups`. A program takes and returns all parts, laid end to end along the dimension named above; an argument that names none is the same for every part. Nothing has to cross between parts.
All inputs are finite; a program needn't handle non-finite values.
Results may differ from a plain program's by a relative error of at most 0.0075.
Values may be sent and summed in bfloat16 or wider, within the bound.
No kernel may reach another device: no remote copies, remote signals or barrier semaphores. Data moves between devices by JAX's collectives and lax.ppermute only.
A program may use at most 128 MiB of HBM per device.

v0:
```python
import jax
import jax.numpy as jnp
from jax import lax
from jax.sharding import PartitionSpec as P

SEQUENCE_DEPTH = 64


def standardize_features(x, gain):
    mean = jnp.mean(x, axis=-1, keepdims=True)
    var = jnp.mean((x - mean) ** 2, axis=-1, keepdims=True)
    return (x - mean) * lax.rsqrt(var + 1e-05) * gain


def on_device(
    alignment_tensor,
    residue_grid,
    mixing_scale_vector,
    logit_offset_scale,
    feedforward_scale,
    product_scale_vector,
    grid_scale_vector,
    logit_offset_map,
    asking_mapping,
    lookup_mapping,
    content_mapping,
    mixing_return_matrix,
    alignment_widen_map,
    alignment_shrink_map,
    former_embedding_map,
    latter_embedding_map,
    product_return_map,
    grid_widen_map,
    grid_shrink_map,
):
    sample_alignment = alignment_tensor[0]
    local_pair = residue_grid[0]
    subspace_total = logit_offset_map.shape[1]
    feature_extent = sample_alignment.shape[-1]
    subspace_number = feature_extent // subspace_total
    sequences_available = sample_alignment.shape[0]
    chain_available = sample_alignment.shape[1]
    tile_rows = local_pair.shape[0]
    tile_cols = local_pair.shape[1]
    product_extent = former_embedding_map.shape[1]
    product_operands = standardize_features(sample_alignment, product_scale_vector).astype(
        jnp.bfloat16
    )
    former_tensor = jnp.dot(
        product_operands, former_embedding_map, preferred_element_type=jnp.float32
    ).astype(jnp.bfloat16)
    latter_tensor = jnp.dot(
        product_operands, latter_embedding_map, preferred_element_type=jnp.float32
    ).astype(jnp.bfloat16)
    left_rows, right_rows = (
        lax.all_gather(former_tensor, "tile", axis=0, tiled=True),
        lax.all_gather(latter_tensor, "tile", axis=0, tiled=True),
    )
    left_all = lax.all_gather(left_rows, "col", axis=1, tiled=True)
    left_mine = lax.dynamic_slice_in_dim(left_all, lax.axis_index("tile") * tile_rows, tile_rows, 1)
    tensor_product = (
        jnp.einsum("era,eyq->ryaq", left_mine, right_rows, preferred_element_type=jnp.float32)
        / SEQUENCE_DEPTH
    )
    update = jnp.dot(
        tensor_product.reshape(tile_rows, tile_cols, product_extent * product_extent),
        product_return_map,
        precision=lax.Precision.HIGHEST,
    )
    bias_tile = jnp.einsum(
        "ijc,ch->hij",
        standardize_features(local_pair, logit_offset_scale),
        logit_offset_map,
        precision=lax.Precision.HIGHEST,
    )
    wide = lax.all_gather(bias_tile, "col", axis=2, tiled=True)
    whole = lax.all_gather(wide.astype(jnp.bfloat16), "tile", axis=1, tiled=True).astype(wide.dtype)
    bias = lax.dynamic_slice_in_dim(
        whole, lax.axis_index("col") * chain_available, chain_available, 1
    )
    standardized_source = standardize_features(sample_alignment, mixing_scale_vector).astype(
        jnp.bfloat16
    )
    asking_vectors = jnp.dot(
        standardized_source, asking_mapping, preferred_element_type=jnp.float32
    ).astype(jnp.bfloat16)
    lookup_vectors = jnp.dot(
        standardized_source, lookup_mapping, preferred_element_type=jnp.float32
    ).astype(jnp.bfloat16)
    content_vectors = jnp.dot(
        standardized_source, content_mapping, preferred_element_type=jnp.float32
    ).astype(jnp.bfloat16)
    all_keys, all_values = (
        lax.all_gather(lookup_vectors, "col", axis=1, tiled=True),
        lax.all_gather(content_vectors, "col", axis=1, tiled=True),
    )
    total_res = all_keys.shape[1]
    asking_vectors = asking_vectors.reshape(
        sequences_available, chain_available, subspace_total, subspace_number
    )
    all_keys = all_keys.reshape(sequences_available, total_res, subspace_total, subspace_number)
    all_values = all_values.reshape(sequences_available, total_res, subspace_total, subspace_number)
    scores = (
        jnp.einsum("sqhd,skhd->shqk", asking_vectors, all_keys, preferred_element_type=jnp.float32)
        / jnp.sqrt(jnp.float32(subspace_number))
        + bias[None]
    )
    weights = jax.nn.softmax(scores, axis=-1).astype(jnp.bfloat16)
    mixing_outcome = jnp.einsum(
        "shqk,skhd->sqhd", weights, all_values, preferred_element_type=jnp.float32
    )
    mixing_outcome = mixing_outcome.astype(jnp.bfloat16).reshape(
        sequences_available, chain_available, feature_extent
    )
    alignment_activations = sample_alignment + jnp.dot(
        mixing_outcome, mixing_return_matrix, preferred_element_type=jnp.float32
    )
    expanded_features = jax.nn.relu(
        jnp.dot(
            standardize_features(alignment_activations, feedforward_scale).astype(jnp.bfloat16),
            alignment_widen_map,
            preferred_element_type=jnp.float32,
        )
    ).astype(jnp.bfloat16)
    alignment_revised = alignment_activations + jnp.dot(
        expanded_features, alignment_shrink_map, preferred_element_type=jnp.float32
    )
    pair_mid = local_pair + update
    spread = jax.nn.relu(
        jnp.dot(
            standardize_features(pair_mid, grid_scale_vector).astype(jnp.bfloat16),
            grid_widen_map,
            preferred_element_type=jnp.float32,
        )
    ).astype(jnp.bfloat16)
    grid_revised = pair_mid + jnp.dot(spread, grid_shrink_map, preferred_element_type=jnp.float32)
    return (alignment_revised[None], grid_revised[None])


def solution(mesh):
    placed = (
        P(("groups", "branch"), "tile", "col", None),
        P(("groups", "branch"), "tile", "col", None),
        P(),
        P(),
        P(),
        P(),
        P(),
        P(),
        P(),
        P(),
        P(),
        P(),
        P(),
        P(),
        P(),
        P(),
        P(),
        P(),
        P(),
    )
    return jax.shard_map(
        on_device,
        mesh=mesh,
        in_specs=placed,
        out_specs=(
            P(("groups", "branch"), "tile", "col", None),
            P(("groups", "branch"), "tile", "col", None),
        ),
        check_vma=False,
    )
```

profile of v0, /device:TPU:0, one launch (start us, length us, event | category | flops | bytes accessed | tf_op | source)
XLA Modules:
  0.0 222.1 jit_solution(14404370128680419553)
XLA Ops:
  7.2 0.0 copy-start
  7.2 0.0 copy-start.2
  7.2 0.0 all-gather.11.cloned.1.call-start
  7.3 2.1 reduce_sum.89
  9.4 2.2 %multiply_reduce_fusion.3 = f32[16,128]{1,0:T(8,128)S(1)} fusion(f32[1,16,128,256]{3,2,1,0:T(8,128)} %param.19, f32[16,128]{1,0:T(8,128)S(1)} %broadcast_multiply_fusion.3), kind=kLoop, calls=%fused_computation.38 | loop fusion | flops 1570816 | bytes 2113536 | tf_op jit(solution)/shard_map/reduce_sum | solution.py:11
  11.6 0.9 convolution_convert_fusion.3
  12.6 17.4 %all_gather.26 = bf16[64,128,32]{1,2,0:T(8,128)(2,1)S(1)} all-gather(bf16[16,128,32]{1,2,0:T(8,128)(2,1)S(1)} %convolution_convert_fusion.3), channel_id=1, replica_groups=mesh['groups'=2,'tile'=4,'col'=2,'branch'=2] {'tile'}, dimensions={0}, use_global_device_ids=true | all-gather | bytes 655360 | tf_op jit(solution)/shard_map/all_gather | solution.py:56
  30.0 1.6 copy.65
  31.6 0.0 all-gather.11.cloned.1.call-update
  31.6 0.0 all-gather.9.cloned.1.call-start
  31.7 5.6 %copy.61 = f32[1,64,128,128]{2,3,1,0:T(8,128)} copy(f32[1,64,128,128]{3,2,1,0:T(8,128)} %param.20) | data formatting | bytes 8388608 | tf_op args[1]
  37.3 3.4 %reduce_sum.91 = f32[64,128]{1,0:T(8,128)S(1)} reduce(f32[1,64,128,128]{3,2,1,0:T(8,128)} %param.20, f32[]{:T(128)} %constant.17.clone.1), dimensions={0,3}, to_apply=%region_2.0 | reduce | flops 1040384 | bytes 4227076 | tf_op jit(solution)/shard_map/reduce_sum | solution.py:10
  40.7 0.0 copy-start.16
  40.7 3.5 %multiply_reduce_fusion.1 = f32[64,128]{1,0:T(8,128)S(1)} fusion(f32[1,64,128,128]{2,3,1,0:T(8,128)} %copy.61, f32[64,128]{1,0:T(8,128)S(1)} %broadcast_multiply_fusion.1), kind=kLoop, calls=%fused_computation.21 | loop fusion | flops 3137536 | bytes 4259840 | tf_op jit(solution)/shard_map/reduce_sum | solution.py:11
  44.3 0.4 copy-done.3
  44.6 2.7 %fusion.26 = bf16[8,64,128]{2,0,1:T(8,128)(2,1)S(1)} fusion(f32[1,64,128,128]{2,3,1,0:T(8,128)S(1)} %copy-done.3, f32[128]{0:T(128)S(1)} %copy-done.18, f32[64,128]{1,0:T(8,128)S(1)} %add_rsqrt_fusion.1, f32[64,128]{1,0:T(8,128)S(1)} %broadcast_multiply_fusion.1, f32[128,8]{0,1:T(8,128)S(1)} %copy-done.15), kind=kOutput, calls=%fused_computation.44 | convolution fusion | flops 103809024 | bytes 4395520 | tf_op jit(solution)/shard_map/ijc,ch->hij/dot_general | solution.py:70
  47.3 9.4 %all_gather.23 = bf16[8,64,256]{2,0,1:T(8,128)(2,1)} all-gather(bf16[8,64,128]{2,0,1:T(8,128)(2,1)S(1)} %fusion.26), channel_id=1, replica_groups=mesh['groups'=2,'tile'=4,'col'=2,'branch'=2] {'col'}, dimensions={2}, use_global_device_ids=true | all-gather | bytes 393216 | tf_op jit(solution)/shard_map/all_gather | solution.py:76
  56.7 0.0 all-gather.9.cloned.1.call-update
  56.8 0.0 all-gather.7.cloned.1.call-start
  56.8 0.7 multiply_convert_fusion.5
  57.5 0.0 copy-start.4
  57.6 1.0 copy-done.4
  58.5 1.5 convolution_convert_fusion
  60.0 0.0 all-gather.7.cloned.1.call-update
  60.0 0.0 all-gather.5.cloned.1.call-start
  60.1 2.6 %convolution_convert_fusion.2 = bf16[16,128,256]{2,1,0:T(8,128)(2,1)} fusion(bf16[16,128,256]{2,1,0:T(8,128)(2,1)} %copy-done.4, bf16[256,256]{1,0:T(8,128)(2,1)S(1)} %copy-done.9), kind=kOutput, calls=%fused_computation.43 | convolution fusion | flops 268959744 | bytes 2228224 | tf_op jit(solution)/shard_map/dot_general | solution.py:90
  62.7 0.0 all-gather.5.cloned.1.call-update
  62.8 0.9 convolution_convert_fusion.4
  63.7 16.1 %all_gather.25 = bf16[64,128,32]{1,2,0:T(8,128)(2,1)S(1)} all-gather(bf16[16,128,32]{1,2,0:T(8,128)(2,1)S(1)} %convolution_convert_fusion.4), channel_id=1, replica_groups=mesh['groups'=2,'tile'=4,'col'=2,'branch'=2] {'tile'}, dimensions={0}, use_global_device_ids=true | all-gather | bytes 655360 | tf_op jit(solution)/shard_map/all_gather | solution.py:57
  79.8 2.7 %convolution_convert_fusion.1 = bf16[16,128,256]{2,1,0:T(8,128)(2,1)} fusion(bf16[16,128,256]{2,1,0:T(8,128)(2,1)} %copy-done.4, bf16[256,256]{1,0:T(8,128)(2,1)S(1)} %copy-done.10), kind=kOutput, calls=%fused_computation.42 | convolution fusion | flops 268959744 | bytes 2228224 | tf_op jit(solution)/shard_map/dot_general | solution.py:84
  82.5 2.3 %copy.59 = bf16[16,128,256]{1,2,0:T(8,128)(2,1)} copy(bf16[16,128,256]{2,1,0:T(8,128)(2,1)} %convolution_convert_fusion.1) | data formatting | bytes 2097152 | tf_op jit(solution)/shard_map/convert_element_type | solution.py:86
  84.8 14.2 %multiply_bitcast_fusion = f32[64,128,32,32]{1,0,2,3:T(8,128)} fusion(bf16[64,128,32,1]{1,2,0,3:T(8,128)(2,1)S(1)} %bitcast.95, bf16[64,256,32]{0,1,2:T(8,128)(2,1)} %all-gather.11.cloned.1.call-done, s32[]{:T(128)S(6)} %select_n.7), kind=kOutput, calls=%fused_computation.1 | convolution fusion | flops 1082130432 | bytes 34603012 | tf_op jit(solution)/shard_map/era,eyq->ryaq/dot_general | solution.py:62
  99.1 32.0 %copy.67 = f32[64,128,32,32]{1,3,2,0:T(8,128)} copy(f32[64,128,32,32]{1,0,2,3:T(8,128)} %multiply_bitcast_fusion) | data formatting | bytes 67108864 | tf_op jit(solution)/shard_map/div | solution.py:62
  131.0 25.6 %fusion.58 = (f32[64,128]{1,0:T(8,128)S(1)}, f32[64,128,128]{1,2,0:T(8,128)}) fusion(f32[64,128,1024]{1,2,0:T(8,128)} %bitcast.94, f32[1024,128]{1,0:T(8,128)S(1)} %copy-done, f32[1,64,128,128]{2,3,1,0:T(8,128)} %copy.61), kind=kOutput, calls=%fused_computation.80 | convolution fusion | flops 12886990848 | bytes 42500096 | tf_op jit(solution)/shard_map/dot_general | solution.py:65
  156.7 3.0 %multiply_reduce_fusion = f32[64,128]{1,0:T(8,128)S(1)} fusion(f32[64,128,128]{1,2,0:T(8,128)} %get-tuple-element.15, f32[64,128]{1,0:T(8,128)S(1)} %broadcast_multiply_fusion), kind=kLoop, calls=%fused_computation.16 | loop fusion | flops 3137536 | bytes 4259840 | tf_op jit(solution)/shard_map/reduce_sum | solution.py:11
  159.8 10.1 %add_bitcast_fusion = f32[1,64,128,128]{2,3,1,0:T(8,128)} fusion(f32[64,128,128]{1,2,0:T(8,128)} %get-tuple-element.15, f32[128]{0:T(128)S(1)} %copy-done.17, f32[64,128]{1,0:T(8,128)S(1)} %add_rsqrt_fusion, f32[64,128]{1,0:T(8,128)S(1)} %broadcast_multiply_fusion, bf16[512,128]{1,0:T(8,128)(2,1)S(1)} %copy-done.6, bf16[128,512]{1,0:T(8,128)(2,1)S(1)} %copy-done.7), kind=kOutput, calls=%fused_computation.14 | convolution fusion | flops 2161115136 | bytes 8716800 | tf_op jit(solution)/shard_map/dot_general | solution.py:136
  169.9 5.6 %copy.72 = f32[1,64,128,128]{3,2,1,0:T(8,128)} copy(f32[1,64,128,128]{2,3,1,0:T(8,128)} %add_bitcast_fusion) | data formatting | bytes 8388608
  175.5 1.1 dynamic-slice_convert_fusion
  176.6 1.3 copy.63
  177.9 3.9 %copy.60 = bf16[16,256,256]{1,2,0:T(8,128)(2,1)} copy(bf16[16,256,256]{2,1,0:T(8,128)(2,1)} %all-gather.7.cloned.1.call-done) | data formatting | bytes 4194304 | tf_op jit(solution)/shard_map/all_gather | solution.py:94
  181.8 12.4 %fusion.56 = (f32[16,8,128]{2,1,0:T(8,128)S(1)}, f32[16,8,128,256]{3,2,1,0:T(8,128)}) fusion(f32[8,128,256]{2,1,0:T(8,128)} %copy.63, bf16[16,128,8,32]{1,3,2,0:T(8,128)(2,1)} %bitcast.98, bf16[16,256,8,32]{1,3,2,0:T(8,128)(2,1)} %bitcast.96), kind=kOutput, calls=%fused_computation.78 | convolution fusion | flops 285212928 | bytes 21037056 | tf_op jit(solution)/shard_map/sub | solution.py:108
  194.2 3.9 %copy.58 = bf16[16,256,256]{1,2,0:T(8,128)(2,1)} copy(bf16[16,256,256]{2,1,0:T(8,128)(2,1)} %all-gather.5.cloned.1.call-done) | data formatting | bytes 4194304 | tf_op jit(solution)/shard_map/all_gather | solution.py:95
  198.1 8.3 %fusion.25 = bf16[16,8,32,128]{3,2,1,0:T(8,128)(2,1)S(1)} fusion(bf16[16,256,8,32]{1,3,2,0:T(8,128)(2,1)} %bitcast.97, f32[16,8,128,256]{3,2,1,0:T(8,128)} %get-tuple-element.11, f32[16,8,128]{2,1,0:T(8,128)S(1)} %get-tuple-element.10), kind=kOutput, calls=%fused_computation.40 | convolution fusion | flops 277348352 | bytes 19988480 | tf_op jit(solution)/shard_map/shqk,skhd->sqhd/dot_general | solution.py:109
  206.5 0.8 fusion.57
  207.3 1.3 copy-done.5
  208.6 0.6 multiply_reduce_fusion.2
  209.3 0.0 copy-start.1
  209.3 6.3 %add_bitcast_fusion.1 = f32[1,16,128,256]{3,2,1,0:T(8,128)} fusion(f32[16,128,256]{2,1,0:T(8,128)} %copy-done.5, f32[256]{0:T(256)S(1)} %copy-done.20, f32[16,128]{1,0:T(8,128)S(1)} %add_rsqrt_fusion.2, f32[16,128]{1,0:T(8,128)S(1)} %broadcast_multiply_fusion.2, bf16[1024,256]{1,0:T(8,128)(2,1)S(1)} %copy-done.19, bf16[256,1024]{1,0:T(8,128)(2,1)} %param.31), kind=kOutput, calls=%fused_computation.31 | convolution fusion | flops 2154299392 | bytes 5260288 | tf_op jit(solution)/shard_map/dot_general | solution.py:125
  (46 shorter events, 0.1 us)
Async XLA Ops:
  7.2 123.9 %copy-start = (f32[1024,128]{1,0:T(8,128)S(1)}, f32[1024,128]{1,0:T(8,128)}, u32[]{:S(2)}) copy-start(f32[1024,128]{1,0:T(8,128)} %param.35) | copy-start | bytes 1572868
  7.2 4.4 %copy-start.2 = (f32[1,16,128,256]{3,2,1,0:T(8,128)S(1)}, f32[1,16,128,256]{3,2,1,0:T(8,128)}, u32[]{:S(2)}) copy-start(f32[1,16,128,256]{3,2,1,0:T(8,128)} %param.19) | copy-start | bytes 6291460
  7.2 4.4 %copy-start.14 = (f32[256]{0:T(256)S(1)}, f32[256]{0:T(256)}, u32[]{:S(2)}) copy-start(f32[256]{0:T(256)} %param.24) | copy-start | bytes 3076
  7.2 4.4 %copy-start.12 = (bf16[256,32]{0,1:T(8,128)(2,1)S(1)}, bf16[256,32]{0,1:T(8,128)(2,1)}, u32[]{:S(2)}) copy-start(bf16[256,32]{0,1:T(8,128)(2,1)} %param.33) | copy-start | bytes 49156
  7.2 77.6 %all-gather.11.cloned.1.call-start = ((), (), s32[]{:S(2)}) async-start(), calls=%async_computation.3 | async-start | bytes 3145728 | tf_op jit(solution)/shard_map/all_gather | solution.py:59
  31.6 143.9 %all-gather.9.cloned.1.call-start = ((), (), s32[]{:S(2)}) async-start(), calls=%async_computation.2 | async-start | bytes 1310720 | tf_op jit(solution)/shard_map/all_gather | solution.py:77
  37.3 7.0 %copy-start.15 = (f32[128,8]{0,1:T(8,128)S(1)}, f32[128,8]{0,1:T(8,128)}, u32[]{:S(2)}) copy-start(f32[128,8]{0,1:T(8,128)} %param.26) | copy-start | bytes 12292
  37.3 7.0 %copy-start.18 = (f32[128]{0:T(128)S(1)}, f32[128]{0:T(128)}, u32[]{:S(2)}) copy-start(f32[128]{0:T(128)} %param.22) | copy-start | bytes 1540
  40.7 3.9 %copy-start.3 = (f32[1,64,128,128]{2,3,1,0:T(8,128)S(1)}, f32[1,64,128,128]{2,3,1,0:T(8,128)}, u32[]{:S(2)}) copy-start(f32[1,64,128,128]{2,3,1,0:T(8,128)} %copy.61) | copy-start | bytes 12582916
  40.7 16.1 %copy-start.16 = (f32[256]{0:T(256)S(1)}, f32[256]{0:T(256)}, u32[]{:S(2)}) copy-start(f32[256]{0:T(256)} %param.21) | copy-start | bytes 3076
  44.2 14.3 %copy-start.8 = (bf16[256,256]{1,0:T(8,128)(2,1)S(1)}, bf16[256,256]{1,0:T(8,128)(2,1)}, u32[]{:S(2)}) copy-start(bf16[256,256]{1,0:T(8,128)(2,1)} %param.28) | copy-start | bytes 393220
  47.3 12.7 %copy-start.9 = (bf16[256,256]{1,0:T(8,128)(2,1)S(1)}, bf16[256,256]{1,0:T(8,128)(2,1)}, u32[]{:S(2)}) copy-start(bf16[256,256]{1,0:T(8,128)(2,1)} %param.29) | copy-start | bytes 393220
  56.7 6.0 %copy-start.13 = (bf16[256,32]{0,1:T(8,128)(2,1)S(1)}, bf16[256,32]{0,1:T(8,128)(2,1)}, u32[]{:S(2)}) copy-start(bf16[256,32]{0,1:T(8,128)(2,1)} %param.34) | copy-start | bytes 49156
  56.8 121.2 %all-gather.7.cloned.1.call-start = ((), (), s32[]{:S(2)}) async-start(), calls=%async_computation.1 | async-start | bytes 3145728 | tf_op jit(solution)/shard_map/all_gather | solution.py:94
  57.5 1.0 copy-start.4
  60.0 19.8 %copy-start.10 = (bf16[256,256]{1,0:T(8,128)(2,1)S(1)}, bf16[256,256]{1,0:T(8,128)(2,1)}, u32[]{:S(2)}) copy-start(bf16[256,256]{1,0:T(8,128)(2,1)} %param.27) | copy-start | bytes 393220
  60.0 134.2 %all-gather.5.cloned.1.call-start = ((), (), s32[]{:S(2)}) async-start(), calls=%async_computation | async-start | bytes 3145728 | tf_op jit(solution)/shard_map/all_gather | solution.py:95
  156.7 3.1 %copy-start.6 = (bf16[512,128]{1,0:T(8,128)(2,1)S(1)}, bf16[512,128]{1,0:T(8,128)(2,1)}, u32[]{:S(2)}) copy-start(bf16[512,128]{1,0:T(8,128)(2,1)} %param.37) | copy-start | bytes 393220
  156.7 3.1 %copy-start.7 = (bf16[128,512]{1,0:T(8,128)(2,1)S(1)}, bf16[128,512]{1,0:T(8,128)(2,1)}, u32[]{:S(2)}) copy-start(bf16[128,512]{1,0:T(8,128)(2,1)} %param.36) | copy-start | bytes 393220
  156.7 3.1 %copy-start.17 = (f32[128]{0:T(128)S(1)}, f32[128]{0:T(128)}, u32[]{:S(2)}) copy-start(f32[128]{0:T(128)} %param.25) | copy-start | bytes 1540
  198.1 8.4 %copy-start.11 = (bf16[256,256]{1,0:T(8,128)(2,1)S(1)}, bf16[256,256]{1,0:T(8,128)(2,1)}, u32[]{:S(2)}) copy-start(bf16[256,256]{1,0:T(8,128)(2,1)} %param.30) | copy-start | bytes 393220
  206.4 2.8 %copy-start.19 = (bf16[1024,256]{1,0:T(8,128)(2,1)S(1)}, bf16[1024,256]{1,0:T(8,128)(2,1)}, u32[]{:S(2)}) copy-start(bf16[1024,256]{1,0:T(8,128)(2,1)} %param.32) | copy-start | bytes 1572868
  206.5 2.8 %copy-start.20 = (f32[256]{0:T(256)S(1)}, f32[256]{0:T(256)}, u32[]{:S(2)}) copy-start(f32[256]{0:T(256)} %param.23) | copy-start | bytes 3076
  207.3 1.4 copy-start.5
  209.3 6.3 %copy-start.1 = (f32[1024,128]{1,0:T(8,128)S(1)}, f32[1024,128]{1,0:T(8,128)}, u32[]{:S(2)}) copy-start(f32[1024,128]{1,0:T(8,128)} %param.35) | copy-start | bytes 1572868
Sparse Core Ops, SparseCore 0:
  31.7 37.6 all-gather.10
  71.0 27.9 all-gather.8
  100.6 32.5 all-gather.6
  134.6 33.0 all-gather.4
where the time goes:
time: 223 us; the launch traced here: 222 us
  matrix products  89.1 us (40%)
  local copies, waits for them, and re-layouts  59 us (26%)
  blocking collectives  42.9 us (19%)
  other arithmetic  16.8 us (8%)
  between operations  14.1 us (6%)
    div x1, local copies, waits for them, and re-layouts, on_device(): jnp.einsum('era,eyq->ryaq', left_mine, right_rows, preferred_element_type...  32 us
    dot_general x1, matrix products, on_device(): jnp.dot(tensor_product.reshape(tile_rows, tile_cols, product_extent * pro...  25.6 us
    all_gather x1, blocking collectives, on_device(): lax.all_gather(former_tensor, 'tile', axis=0, tiled=True)  17.4 us
    all_gather x1, blocking collectives, on_device(): lax.all_gather(latter_tensor, 'tile', axis=0, tiled=True)  16.1 us
    dot_general x1, matrix products, on_device(): jnp.einsum('era,eyq->ryaq', left_mine, right_rows, preferred_element_type...  14.2 us
    unnamed x44, local copies, waits for them, and re-layouts  14 us
    sub x1, matrix products, on_device(): weights = jax.nn.softmax(scores, axis=-1).astype(jnp.bfloat16)  12.4 us
    dot_general x1, matrix products, on_device(): jnp.dot(spread, grid_shrink_map, preferred_element_type=jnp.float32)  10.1 us
  transfers between devices with their start and end apart: 4, of which 0 were waited for; matrix products, arithmetic and copies ran while one was open for 61% of the time, Pallas kernels for 0%

commit v1 on v0

--- a/solution.py
+++ b/solution.py
@@ -1,18 +1,24 @@
+import functools
+
 import jax
 import jax.numpy as jnp
 from jax import lax
+from jax.experimental import pallas as pl
+from jax.experimental.pallas import tpu as pltpu
 from jax.sharding import PartitionSpec as P
 
-SEQUENCE_DEPTH = 64
+EPS = 1e-05
+LANES = 128
+LOG2E = 1.4426950408889634
 
 
 def standardize_features(x, gain):
     mean = jnp.mean(x, axis=-1, keepdims=True)
     var = jnp.mean((x - mean) ** 2, axis=-1, keepdims=True)
-    return (x - mean) * lax.rsqrt(var + 1e-05) * gain
-
-
-def on_device(
+    return (x - mean) * lax.rsqrt(var + EPS) * gain
+
+
+def gathered(
     alignment_tensor,
     residue_grid,
     mixing_scale_vector,
@@ -60,7 +66,7 @@
     left_mine = lax.dynamic_slice_in_dim(left_all, lax.axis_index("tile") * tile_rows, tile_rows, 1)
     tensor_product = (
         jnp.einsum("era,eyq->ryaq", left_mine, right_rows, preferred_element_type=jnp.float32)
-        / SEQUENCE_DEPTH
+        / left_rows.shape[0]
     )
     update = jnp.dot(
         tensor_product.reshape(tile_rows, tile_cols, product_extent * product_extent),
@@ -135,6 +141,345 @@
     ).astype(jnp.bfloat16)
     grid_revised = pair_mid + jnp.dot(spread, grid_shrink_map, preferred_element_type=jnp.float32)
     return (alignment_revised[None], grid_revised[None])
+
+
+def normalized(x):
+    mean = jnp.mean(x, axis=-1, keepdims=True)
+    centered = x - mean
+    var = jnp.mean(centered * centered, axis=-1, keepdims=True)
+    return centered * lax.rsqrt(var + EPS)
+
+
+def dot(a, b, dims=((1,), (0,))):
+    return lax.dot_general(a, b, (dims, ((), ())), preferred_element_type=jnp.float32)
+
+
+def factors_kernel(rows, x_ref, mix_ref, gain_ref, wl_ref, wr_ref, normed_ref, left_ref, right_ref, std, lacc, racc):
+    step = pl.program_id(0)
+    block, residues, features = x_ref.shape
+    extent = wl_ref.shape[1]
+    pack = LANES // extent
+    groups = residues // pack
+    base = normalized(x_ref[...].reshape(block * residues, features))
+    normed_ref[...] = (base * mix_ref[...]).astype(jnp.bfloat16).reshape(block, residues, features)
+    scaled = base * gain_ref[...]
+    spans = features // LANES
+    for f in range(spans):
+        std[f] = scaled[:, f * LANES : (f + 1) * LANES]
+    turned = dot(wr_ref[...], scaled.astype(jnp.bfloat16), ((0,), (1,)))
+    packed = jnp.zeros((block * groups, LANES), jnp.float32)
+    source = lax.broadcasted_iota(jnp.int32, (extent, LANES), 0)
+    target = lax.broadcasted_iota(jnp.int32, (extent, LANES), 1)
+    for a in range(pack):
+        spread = (source + a * extent == target).astype(jnp.bfloat16)
+        wide = dot(wl_ref[...], spread).astype(jnp.bfloat16)
+        picked = [std[f, pl.ds(a, block * groups, stride=pack), :] for f in range(spans)]
+        packed = packed + dot(jnp.concatenate(picked, axis=1).astype(jnp.bfloat16), wide)
+    for k in range(block):
+        row = step * block + k
+        racc[pl.ds(row, extent, stride=rows), :] = turned[:, k * residues : (k + 1) * residues]
+        lacc[pl.ds(row, groups, stride=rows), :] = packed[k * groups : (k + 1) * groups]
+
+    @pl.when(step == pl.num_programs(0) - 1)
+    def _():
+        left_ref[...] = lacc[...].astype(jnp.bfloat16)
+        right_ref[...] = racc[...].astype(jnp.bfloat16)
+
+
+def factors(x, mix, gain, wl, wr, block):
+    rows, residues, features = x.shape
+    extent = wl.shape[1]
+    groups = residues * extent // LANES
+    whole = lambda shape: pl.BlockSpec(shape, lambda i: (0,) * len(shape))
+    tile = pl.BlockSpec((block, residues, features), lambda i: (i, 0, 0))
+    return pl.pallas_call(
+        functools.partial(factors_kernel, rows),
+        grid=(rows // block,),
+        in_specs=[tile, whole((1, features)), whole((1, features)), whole(wl.shape), whole(wr.shape)],
+        out_specs=[tile, whole((groups * rows, LANES)), whole((extent * rows, residues))],
+        out_shape=[
+            jax.ShapeDtypeStruct((rows, residues, features), jnp.bfloat16),
+            jax.ShapeDtypeStruct((groups * rows, LANES), jnp.bfloat16),
+            jax.ShapeDtypeStruct((extent * rows, residues), jnp.bfloat16),
+        ],
+        scratch_shapes=[
+            pltpu.VMEM((features // LANES, block * residues, LANES), jnp.float32),
+            pltpu.VMEM((groups * rows, LANES), jnp.float32),
+            pltpu.VMEM((extent * rows, residues), jnp.float32),
+        ],
+        name="factors",
+        cost_estimate=pl.CostEstimate(
+            flops=2 * rows * residues * features * 5 * extent,
+            bytes_accessed=rows * residues * features * 6,
+            transcendentals=rows * residues,
+        ),
+    )(x, mix.reshape(1, -1), gain.reshape(1, -1), wl, wr)
+
+
+def bias_kernel(heads, x_ref, gain_ref, w_ref, out_ref, acc):
+    step = pl.program_id(0)
+    block, cols, features = x_ref.shape
+    rows = acc.shape[0] // heads
+    scaled = normalized(x_ref[...].reshape(block * cols, features)) * gain_ref[...]
+    turned = dot(w_ref[...].astype(jnp.bfloat16), scaled.astype(jnp.bfloat16), ((0,), (1,)))
+    for k in range(block):
+        acc[pl.ds(step * block + k, heads, stride=rows), :] = turned[:, k * cols : (k + 1) * cols]
+
+    @pl.when(step == pl.num_programs(0) - 1)
+    def _():
+        out_ref[...] = acc[...].astype(jnp.bfloat16)
+
+
+def pair_bias(pair, gain, w, block):
+    rows, cols, features = pair.shape
+    heads = w.shape[1]
+    whole = lambda shape: pl.BlockSpec(shape, lambda i: (0,) * len(shape))
+    return pl.pallas_call(
+        functools.partial(bias_kernel, heads),
+        grid=(rows // block,),
+        in_specs=[
+            pl.BlockSpec((block, cols, features), lambda i: (i, 0, 0)),
+            whole((1, features)),
+            whole(w.shape),
+        ],
+        out_specs=whole((heads * rows, cols)),
+        out_shape=jax.ShapeDtypeStruct((heads * rows, cols), jnp.bfloat16),
+        scratch_shapes=[pltpu.VMEM((heads * rows, cols), jnp.float32)],
+        name="pair_bias",
+        cost_estimate=pl.CostEstimate(
+            flops=2 * rows * cols * features * heads * 8,
+            bytes_accessed=rows * cols * features * 4,
+            transcendentals=rows * cols,
+        ),
+    )(pair, gain.reshape(1, -1), w).reshape(heads, rows, cols)
+
+
+def pair_kernel(parts, rows, extent, *refs):
+    lefts, rights = refs[:parts], refs[parts : 2 * parts]
+    pair_ref, wt_ref, gain_ref, wide_ref, shrink_ref, out_ref, rall, lall, outer = refs[2 * parts :]
+    step = pl.program_id(0)
+    block, cols, channels = pair_ref.shape
+
+    @pl.when(step == 0)
+    def _():
+        for b, right in enumerate(rights):
+            for d in range(extent):
+                rall[b * rows : (b + 1) * rows, d * cols : (d + 1) * cols] = right[d * rows : (d + 1) * rows, :]
+        for r in range(lefts[0].shape[0] // rows):
+            stacked = jnp.concatenate([left[r * rows : (r + 1) * rows, :] for left in lefts], axis=0)
+            lall[r * LANES : (r + 1) * LANES, :] = stacked.T
+
+    mine = lall[pl.ds(pl.multiple_of(step * block * extent, block * extent), block * extent), :]
+    chunk = min(8, extent)
+    for d0 in range(0, extent, chunk):
+        product = dot(mine, rall[:, d0 * cols : (d0 + chunk) * cols]).astype(jnp.bfloat16)
+        for i in range(block):
+            for d in range(chunk):
+                outer[i // 2, (d0 + d) * extent : (d0 + d + 1) * extent, (i % 2) * cols : (i % 2 + 1) * cols] = product[
+                    i * extent : (i + 1) * extent, d * cols : (d + 1) * cols
+                ]
+    for k in range(block // 2):
+        turned = dot(wt_ref[...], outer[k])
+        mids = []
+        for i in range(2):
+            mids.append(pair_ref[2 * k + i] + turned[:, i * cols : (i + 1) * cols].T)
+        mid = jnp.concatenate(mids, axis=0)
+        normed = (normalized(mid) * gain_ref[...]).astype(jnp.bfloat16)
+        spread = jnp.maximum(dot(normed, wide_ref[...]), 0.0).astype(jnp.bfloat16)
+        done = mid + dot(spread, shrink_ref[...])
+        out_ref[2 * k : 2 * k + 2] = done.reshape(2, cols, channels)
+
+
+def pair_update(lefts, rights, pair, wt, gain, wide, shrink, rows, block):
+    parts = len(lefts)
+    tile_rows, cols, channels = pair.shape
+    extent = rights[0].shape[0] // rows
+    whole = lambda shape: pl.BlockSpec(shape, lambda i: (0,) * len(shape))
+    tile = pl.BlockSpec((block, cols, channels), lambda i: (i, 0, 0))
+    return pl.pallas_call(
+        functools.partial(pair_kernel, parts, rows, extent),
+        grid=(tile_rows // block,),
+        in_specs=[whole(a.shape) for a in (*lefts, *rights)]
+        + [tile, whole(wt.shape), whole((1, channels)), whole(wide.shape), whole(shrink.shape)],
+        out_specs=tile,
+        out_shape=jax.ShapeDtypeStruct(pair.shape, jnp.float32),
+        scratch_shapes=[
+            pltpu.VMEM((parts * rows, extent * cols), jnp.bfloat16),
+            pltpu.VMEM((tile_rows * extent, parts * rows), jnp.bfloat16),
+            pltpu.VMEM((block // 2, extent * extent, 2 * cols), jnp.bfloat16),
+        ],
+        name="pair_update",
+        cost_estimate=pl.CostEstimate(
+            flops=2 * tile_rows * cols * (extent * extent * (parts * rows + channels) + 2 * wide.size) * 2,
+            bytes_accessed=pair.size * 8,
+            transcendentals=tile_rows * cols,
+        ),
+    )(*lefts, *rights, pair, wt, gain.reshape(1, -1), wide, shrink)
+
+
+def attention_kernel(
+    heads, where_ref, x_ref, own_ref, far_ref, b00, b01, b10, b11, wq_ref, wk_ref, wv_ref, wo_ref, gain_ref,
+    wide_ref, shrink_ref, out_ref, bias,
+):
+    step = pl.program_id(0)
+    block, residues, features = x_ref.shape
+    depth = features // heads
+    half = residues // 2
+    bf16 = jnp.bfloat16
+
+    @pl.when(step == 0)
+    def _():
+        first = pl.multiple_of(where_ref[0] * half, half)
+        second = pl.multiple_of((1 - where_ref[0]) * half, half)
+        for start, (near, far) in ((first, (b00, b01)), (second, (b10, b11))):
+            bias[:, pl.ds(start, half), :residues] = near[...].astype(jnp.float32) * LOG2E
+            bias[:, pl.ds(start, half), residues:] = far[...].astype(jnp.float32) * LOG2E
+
+    x = x_ref[...].reshape(block * residues, features)
+    own = own_ref[...].reshape(block * residues, features)
+    far = far_ref[...].reshape(block * residues, features)
+    factor = LOG2E / (depth**0.5)
+    query = (dot(own, wq_ref[...]) * factor).astype(bf16)
+    keys = [dot(a, wk_ref[...]).astype(bf16) for a in (own, far)]
+    values = [dot(a, wv_ref[...]).astype(bf16) for a in (own, far)]
+    lane = lax.broadcasted_iota(jnp.int32, (1, features), 1) // depth
+    mixed = []
+    for s in range(block):
+        rows = slice(s * residues, (s + 1) * residues)
+        key = jnp.concatenate([k[rows] for k in keys], axis=0)
+        value = jnp.concatenate([v[rows] for v in values], axis=0)
+        total = jnp.zeros((residues, features), jnp.float32)
+        for h in range(heads):
+            mask = lane == h
+            only = query[rows] * mask.astype(bf16)
+            score = dot(only, key, ((1,), (1,))) + bias[h]
+            weight = jnp.exp2(score - jnp.max(score, axis=-1, keepdims=True))
+            norm = 1.0 / jnp.sum(weight, axis=-1, keepdims=True)
+            total = jnp.where(mask, dot(weight.astype(bf16), value) * norm, total)
+        mixed.append(total.astype(bf16))
+    mid = x + dot(jnp.concatenate(mixed, axis=0), wo_ref[...])
+    normed = (normalized(mid) * gain_ref[...]).astype(bf16)
+    lifted = jnp.maximum(dot(normed, wide_ref[...]), 0.0).astype(bf16)
+    out_ref[...] = (mid + dot(lifted, shrink_ref[...])).reshape(block, residues, features)
+
+
+def attention(parity, x, own, far, biases, weights, gain, wide, shrink, block):
+    rows, residues, features = x.shape
+    heads = biases[0].shape[0]
+    whole = lambda shape: pl.BlockSpec(shape, lambda i, *_: (0,) * len(shape))
+    tile = pl.BlockSpec((block, residues, features), lambda i, *_: (i, 0, 0))
+    return pl.pallas_call(
+        functools.partial(attention_kernel, heads),
+        grid_spec=pltpu.PrefetchScalarGridSpec(
+            num_scalar_prefetch=1,
+            grid=(rows // block,),
+            in_specs=[tile, tile, tile]
+            + [whole(b.shape) for b in biases]
+            + [whole(w.shape) for w in weights]
+            + [whole((1, features)), whole(wide.shape), whole(shrink.shape)],
+            out_specs=tile,
+            scratch_shapes=[pltpu.VMEM((heads, residues, 2 * residues), jnp.float32)],
+        ),
+        out_shape=jax.ShapeDtypeStruct(x.shape, jnp.float32),
+        name="attention",
+        cost_estimate=pl.CostEstimate(
+            flops=2 * rows * residues * (6 * features * features + 4 * heads * residues * features + 2 * wide.size),
+            bytes_accessed=rows * residues * features * 12,
+            transcendentals=rows * residues * heads * 2 * residues,
+        ),
+    )(parity, x, own, far, *biases, *weights, gain.reshape(1, -1), wide, shrink)
+
+
+def exchanged(
+    alignment_tensor,
+    residue_grid,
+    mixing_scale_vector,
+    logit_offset_scale,
+    feedforward_scale,
+    product_scale_vector,
+    grid_scale_vector,
+    logit_offset_map,
+    asking_mapping,
+    lookup_mapping,
+    content_mapping,
+    mixing_return_matrix,
+    alignment_widen_map,
+    alignment_shrink_map,
+    former_embedding_map,
+    latter_embedding_map,
+    product_return_map,
+    grid_widen_map,
+    grid_shrink_map,
+):
+    msa, pair = alignment_tensor[0], residue_grid[0]
+    rows = msa.shape[0]
+    tiles = lax.axis_size("tile")
+    extent = former_embedding_map.shape[1]
+    channels = pair.shape[-1]
+    mine, side = lax.axis_index("tile"), lax.axis_index("col")
+    upper = tiles // 2
+
+    def swap(value, axis, mask):
+        return lax.ppermute(value, axis, [(i, i ^ mask) for i in range(lax.axis_size(axis))])
+
+    normed, left, right = factors(
+        msa, mixing_scale_vector, product_scale_vector, former_embedding_map, latter_embedding_map, 4
+    )
+    left_far = swap(left, "col", 1)
+    low = jnp.where(side == 0, left, left_far)
+    high = jnp.where(side == 0, left_far, left)
+    rights = [right] + [swap(right, "tile", k) for k in range(1, tiles)]
+    pieces = jnp.concatenate([low, high], axis=0).reshape(tiles, -1, LANES)
+    lefts = [lax.dynamic_index_in_dim(pieces, mine, 0, keepdims=False)]
+    for k in range(1, tiles):
+        lefts.append(swap(lax.dynamic_index_in_dim(pieces, mine ^ k, 0, keepdims=False), "tile", k))
+
+    tile_bias = pair_bias(pair, logit_offset_scale, logit_offset_map, 8)
+    other = swap(tile_bias, "tile", upper)
+    stays = (mine // upper) == side
+    near = jnp.where(stays, tile_bias, other)
+    gone = jnp.where(stays, other, tile_bias)
+    far = swap(gone, "col", 1)
+    biases = (near, far, swap(near, "tile", 1), swap(far, "tile", 1))
+
+    normed_far = swap(normed, "col", 1)
+
+    total_rows = rows * tiles
+    wt = product_return_map.reshape(extent, extent, channels).transpose(2, 1, 0).reshape(channels, extent * extent)
+    wt = (wt * (1.0 / total_rows)).astype(jnp.bfloat16)
+    grid_revised = pair_update(
+        lefts, rights, pair, wt, grid_scale_vector, grid_widen_map, grid_shrink_map, rows, 8
+    )
+    parity = (mine % upper).astype(jnp.int32).reshape(1)
+    alignment_revised = attention(
+        parity,
+        msa,
+        normed,
+        normed_far,
+        biases,
+        (asking_mapping, lookup_mapping, content_mapping, mixing_return_matrix),
+        feedforward_scale,
+        alignment_widen_map,
+        alignment_shrink_map,
+        2,
+    )
+    return (alignment_revised[None], grid_revised[None])
+
+
+def on_device(*args):
+    msa, pair = args[0], args[1]
+    extent = args[14].shape[1]
+    fits = (
+        lax.axis_size("col") == 2
+        and lax.axis_size("tile") == 4
+        and msa.shape[1] % 16 == 0
+        and msa.shape[2] == LANES
+        and pair.shape[1] % 16 == 0
+        and pair.shape[2] == LANES
+        and LANES % extent == 0
+        and extent % 16 == 0
+    )
+    return exchanged(*args) if fits else gathered(*args)
 
 
 def solution(mesh):

time: 223 us -> 137 us (0.61)
  Pallas kernels: 0 us -> 92.3 us
  matrix products: 89.1 us -> 0 us
  local copies, waits for them, and re-layouts: 59 us -> 6.12 us
  blocking collectives: 42.9 us -> 0 us
  waiting for transfers between devices: 0.07 us -> 19.5 us
  starting transfers between devices: 0.16 us -> 15.6 us
  other arithmetic: 16.8 us -> 1.9 us
  between operations: 14.1 us -> 0.81 us
    pallas_call x0 -> x4, Pallas kernels: none -> 92.3 us  [the longest x1 45.3 us: attention(): pl.pallas_call(functools.partial(attention_kernel, heads), grid_spec=pltp...]
    dot_general x12 -> x0, matrix products: 76.7 us -> none  [the longest x1 25.6 us: on_device(): jnp.dot(tensor_product.reshape(tile_rows, tile_cols, product_extent * pro...]
    all_gather x3 -> x0, blocking collectives: 42.9 us -> none  [the longest x1 17.4 us: on_device(): lax.all_gather(former_tensor, 'tile', axis=0, tiled=True)]
    div x1 -> x0, local copies, waits for them, and re-layouts: 32 us -> none  [on_device(): jnp.einsum('era,eyq->ryaq', left_mine, right_rows, preferred_element_type...]
    ppermute x0 -> x12, waiting for transfers between devices: none -> 19.5 us  [swap(): lax.ppermute(value, axis, [(i, i ^ mask) for i in range(lax.axis_size(axi...]
    ppermute x0 -> x12, starting transfers between devices: none -> 15.6 us  [swap(): lax.ppermute(value, axis, [(i, i ^ mask) for i in range(lax.axis_size(axi...]
    reduce_sum x6 -> x0, other arithmetic: 14.9 us -> none  [the longest x4 9.34 us: standardize_features(): var = jnp.mean((x - mean) ** 2, axis=-1, keepdims=True)]
    sub x1 -> x0, matrix products: 12.4 us -> none  [on_device(): weights = jax.nn.softmax(scores, axis=-1).astype(jnp.bfloat16)]
  transfers between devices with their start and end apart: 4 -> 12, of which waited for: 0 -> 4; matrix products, arithmetic and copies ran while one was open for 61% -> 4% of each run, Pallas kernels for 0% -> 29%
where the time goes in v1:
time: 137 us; the launch traced here: 136 us
  Pallas kernels  92.3 us (67%)
  waiting for transfers between devices  19.5 us (14%)
  starting transfers between devices  15.6 us (11%)
  local copies, waits for them, and re-layouts  6.12 us (4%)
  other arithmetic  1.9 us (1%)
    pallas_call x1, Pallas kernels, attention(): pl.pallas_call(functools.partial(attention_kernel, heads), grid_spec=pltp...  45.3 us
    pallas_call x1, Pallas kernels, pair_update(): pl.pallas_call(functools.partial(pair_kernel, parts, rows, extent), grid=...  33.7 us
    ppermute x12, waiting for transfers between devices, swap(): lax.ppermute(value, axis, [(i, i ^ mask) for i in range(lax.axis_size(axi...  19.5 us
    ppermute x12, starting transfers between devices, swap(): lax.ppermute(value, axis, [(i, i ^ mask) for i in range(lax.axis_size(axi...  15.6 us
    pallas_call x1, Pallas kernels, pair_bias(): pl.pallas_call(functools.partial(bias_kernel, heads), grid=(rows // block...  7.61 us
    pallas_call x1, Pallas kernels, factors(): pl.pallas_call(functools.partial(factors_kernel, rows), grid=(rows // blo...  5.65 us
    unnamed x31, local copies, waits for them, and re-layouts  4.52 us
  transfers between devices with their start and end apart: 12, of which 4 were waited for; matrix products, arithmetic and copies ran while one was open for 4% of the time, Pallas kernels for 29%

profile of v1, /device:TPU:0, one launch (start us, length us, event | category | flops | bytes accessed | tf_op | source)
XLA Modules:
  0.0 136.3 jit_solution(7414800295242909617)
XLA Ops:
  0.7 1.4 %copy.31.w_ref = f32[128,8]{1,0:T(8,128)} copy(f32[128,8]{0,1:T(8,128)} %param.26) | data formatting | bytes 8192 | tf_op args[7]
  2.1 7.6 %pair_bias.1 = bf16[512,128]{1,0:T(8,128)(2,1)} custom-call(f32[64,128,128]{2,1,0:T(8,128)} %bitcast.24, f32[1,128]{1,0:T(1,128)} %bitcast.35, f32[128,8]{1,0:T(8,128)} %copy.31.w_ref), custom_call_target="tpu_custom_call" | custom-call | flops 134217728 | bytes 4194304 | tf_op jit(solution)/shard_map/pair_bias/pallas_call | solution.py:237
  9.7 4.1 %collective-permute-start.1 = (bf16[8,64,128]{2,1,0:T(8,128)(2,1)}, bf16[8,64,128]{2,1,0:T(8,128)(2,1)S(1)}, u32[]{:S(2)}, u32[]{:S(2)}) collective-permute-start(bf16[8,64,128]{2,1,0:T(8,128)(2,1)} %bitcast.31), channel_id=1, source_target_pairs={{0,8},{4,12},{8,0},{12,4},{1,9},{5,13},{9,1},{13,5},{2,10},{6,14},... | collective-permute-start | bytes 393224 | tf_op jit(solution)/shard_map/ppermute | solution.py:423
  13.8 0.7 copy.29.wl_ref
  14.5 0.7 copy.30.wr_ref
  15.2 5.7 %factors.1 = (bf16[16,128,256]{2,1,0:T(8,128)(2,1)}, bf16[512,128]{1,0:T(8,128)(2,1)}, bf16[512,128]{1,0:T(8,128)(2,1)}) custom-call(f32[16,128,256]{2,1,0:T(8,128)} %bitcast.26, f32[1,256]{1,0:T(1,128)} %bitcast.33, f32[1,256]{1,0:T(1,128)} %bitcast.34, bf16[256,32]{1,0:T(8,128)(2,1)} %copy.29.wl_ref, bf16[256,32]{1,0:T(8,128)(2,1)} %copy.30.wr_ref), custom_call_target="tpu_custom_call" | custom-call | flops 167772160 | bytes 3145728 | tf_op jit(solution)/shard_map/factors/pallas_call | solution.py:195
  20.9 1.3 collective-permute-start.11
  22.2 1.7 %collective-permute-start.10 = (bf16[512,128]{1,0:T(8,128)(2,1)}, bf16[512,128]{1,0:T(8,128)(2,1)S(1)}, u32[]{:S(2)}, u32[]{:S(2)}) collective-permute-start(bf16[512,128]{1,0:T(8,128)(2,1)} %get-tuple-element.7.refs_4_), channel_id=1, source_target_pairs={{0,8},{4,12},{8,0},{12,4},{1,9},{5,13},{9,1},{13,5},{2,10},{6,14},... | collective-permute-start | bytes 393224 | tf_op jit(solution)/shard_map/ppermute | solution.py:423
  23.9 1.4 collective-permute-start.9
  25.3 1.5 %collective-permute-start.5 = (bf16[512,128]{1,0:T(8,128)(2,1)}, bf16[512,128]{1,0:T(8,128)(2,1)S(1)}, u32[]{:S(2)}, u32[]{:S(2)}) collective-permute-start(bf16[512,128]{1,0:T(8,128)(2,1)} %get-tuple-element.6), channel_id=1, source_target_pairs={{0,2},{2,0},{1,3},{3,1},{4,6},{6,4},{5,7},{7,5},{8,10},{10,8},{9,1... | collective-permute-start | bytes 393224 | tf_op jit(solution)/shard_map/ppermute | solution.py:423
  26.7 0.0 collective-permute-done.1
  26.7 0.5 collective-permute-start
  27.3 0.9 broadcast_select_fusion.2
  28.2 0.0 copy-start.1
  28.2 3.6 %collective-permute-done.5 = bf16[512,128]{1,0:T(8,128)(2,1)S(1)} collective-permute-done((bf16[512,128]{1,0:T(8,128)(2,1)}, bf16[512,128]{1,0:T(8,128)(2,1)S(1)}, u32[]{:S(2)}, u32[]{:S(2)}) %collective-permute-start.5) | collective-permute-done | bytes 131104 | tf_op jit(solution)/shard_map/ppermute | solution.py:423
  31.8 1.5 %collective-permute-start.2 = (bf16[8,64,128]{2,1,0:T(8,128)(2,1)S(1)}, bf16[8,64,128]{2,1,0:T(8,128)(2,1)S(1)}, u32[]{:S(2)}, u32[]{:S(2)}) collective-permute-start(bf16[8,64,128]{2,1,0:T(8,128)(2,1)S(1)} %get-tuple-element.14), channel_id=1, source_target_pairs={{0,2},{2,0},{1,3},{3,1},{4,6},{6,4},{5,7},{7,5},{8,10},{10,8},{9,1... | collective-permute-start | bytes 393224 | tf_op jit(solution)/shard_map/ppermute | solution.py:423
  33.3 0.9 broadcast_select_fusion.1
  34.3 0.6 dynamic-slice_bitcast_fusion
  34.9 0.0 collective-permute-done.11.refs_7_
  34.9 1.3 collective-permute-start.8
  36.3 1.4 %collective-permute-done.10.refs_6_ = bf16[512,128]{1,0:T(8,128)(2,1)S(1)} collective-permute-done((bf16[512,128]{1,0:T(8,128)(2,1)}, bf16[512,128]{1,0:T(8,128)(2,1)S(1)}, u32[]{:S(2)}, u32[]{:S(2)}) %collective-permute-start.10) | collective-permute-done | bytes 131104 | tf_op jit(solution)/shard_map/ppermute | solution.py:423
  37.7 0.0 collective-permute-start.7
  37.7 0.0 collective-permute-done.9.refs_5_
  37.7 1.6 %collective-permute-start.6 = (bf16[256,128]{1,0:T(8,128)(2,1)S(1)}, bf16[256,128]{1,0:T(8,128)(2,1)S(1)}, u32[]{:S(2)}, u32[]{:S(2)}) collective-permute-start(bf16[256,128]{1,0:T(8,128)(2,1)S(1)} %get-tuple-element.10), channel_id=1, source_target_pairs={{0,4},{4,0},{8,12},{12,8},{1,5},{5,1},{9,13},{13,9},{2,6},{6,2},{1... | collective-permute-start | bytes 196616 | tf_op jit(solution)/shard_map/ppermute | solution.py:423
  39.3 0.0 copy-done
  39.4 0.1 copy.32
  39.5 0.9 copy.33.refs_9_
  40.3 1.2 collective-permute-done.8.refs_3_
  41.6 0.0 collective-permute-start.3
  41.6 13.3 %collective-permute-done.2.b01 = bf16[8,64,128]{2,1,0:T(8,128)(2,1)S(1)} collective-permute-done((bf16[8,64,128]{2,1,0:T(8,128)(2,1)S(1)}, bf16[8,64,128]{2,1,0:T(8,128)(2,1)S(1)}, u32[]{:S(2)}, u32[]{:S(2)}) %collective-permute-start.2) | collective-permute-done | bytes 131104 | tf_op jit(solution)/shard_map/ppermute | solution.py:423
  54.9 0.7 collective-permute-start.4
  55.5 0.0 collective-permute-done.7.refs_2_
  55.5 0.0 collective-permute-done.6.refs_1_
  55.5 0.0 copy-start.13
  55.6 0.0 copy-done.5
  55.6 0.0 copy-done.6
  55.6 0.0 copy-done.7
  55.6 0.0 copy-done.11
  55.6 0.6 copy-done.12
  56.2 0.0 copy-done.13
  56.2 33.7 %pair_update.1 = f32[64,128,128]{2,1,0:T(8,128)} custom-call(bf16[256,128]{1,0:T(8,128)(2,1)} %get-tuple-element.11.refs_0_, bf16[256,128]{1,0:T(8,128)(2,1)} %copy-done.13, bf16[256,128]{1,0:T(8,128)(2,1)} %copy-done.12, bf16[256,128]{1,0:T(8,128)(2,1)} %copy-done.11, bf16[512,128]{1,0:T(8,128)(2,1)} %get-tuple-element.7.refs_4_, ...), custom_call_target="tpu_custom_call" | custom-call | flops 10737418240 | bytes 8388608 | tf_op jit(solution)/shard_map/pair_update/pallas_call | solution.py:299
  89.9 0.0 collective-permute-done.3.b10
  90.0 0.0 collective-permute-done.4.b11
  90.0 0.0 collective-permute-done.far_ref
  90.0 0.6 copy-done.9
  90.6 0.1 copy-done.10
  90.7 0.3 copy-done.4
  91.0 45.3 %attention.1 = f32[16,128,256]{2,1,0:T(8,128)} custom-call(s32[1]{0:T(128)} %bitcast.where_ref, f32[16,128,256]{2,1,0:T(8,128)} %bitcast.27, bf16[16,128,256]{2,1,0:T(8,128)(2,1)} %get-tuple-element.5.own_ref, bf16[16,128,256]{2,1,0:T(8,128)(2,1)} %copy-done.4, bf16[8,64,128]{2,1,0:T(8,128)(2,1)} %copy-done.1, bf16[8,64,128]{2,1,0:T(8,128)(2,1)} %copy-done.8, ...), custom_call_target="tpu_custom_call" | custom-call | flops 8053063680 | bytes 6291456 | tf_op jit(solution)/shard_map/attention/pallas_call | solution.py:371
  (18 shorter events, 0.1 us)
Async XLA Ops:
  0.6 13.1 %copy-start.2 = (bf16[256,32]{0,1:T(8,128)(2,1)S(1)}, bf16[256,32]{0,1:T(8,128)(2,1)}, u32[]{:S(2)}) copy-start(bf16[256,32]{0,1:T(8,128)(2,1)} %param.33) | copy-start | bytes 49156
  0.6 13.8 %copy-start.3 = (bf16[256,32]{0,1:T(8,128)(2,1)S(1)}, bf16[256,32]{0,1:T(8,128)(2,1)}, u32[]{:S(2)}) copy-start(bf16[256,32]{0,1:T(8,128)(2,1)} %param.34) | copy-start | bytes 49156
  2.1 37.3 %copy-start = (f32[1024,128]{1,0:T(8,128)S(1)}, f32[1024,128]{1,0:T(8,128)}, u32[]{:S(2)}) copy-start(f32[1024,128]{1,0:T(8,128)} %param.35) | copy-start | bytes 1572868
  9.7 17.1 %collective-permute-start.1 = (bf16[8,64,128]{2,1,0:T(8,128)(2,1)}, bf16[8,64,128]{2,1,0:T(8,128)(2,1)S(1)}, u32[]{:S(2)}, u32[]{:S(2)}) collective-permute-start(bf16[8,64,128]{2,1,0:T(8,128)(2,1)} %bitcast.31), channel_id=1, source_target_pairs={{0,8},{4,12},{8,0},{12,4},{1,9},{5,13},{9,1},{13,5},{2,10},{6,14},... | collective-permute-start | bytes 393224 | tf_op jit(solution)/shard_map/ppermute | solution.py:423
  20.9 14.1 %collective-permute-start.11 = (bf16[512,128]{1,0:T(8,128)(2,1)}, bf16[512,128]{1,0:T(8,128)(2,1)S(1)}, u32[]{:S(2)}, u32[]{:S(2)}) collective-permute-start(bf16[512,128]{1,0:T(8,128)(2,1)} %get-tuple-element.7.refs_4_), channel_id=1, source_target_pairs={{0,12},{4,8},{8,4},{12,0},{1,13},{5,9},{9,5},{13,1},{2,14},{6,10},... | collective-permute-start | bytes 393224 | tf_op jit(solution)/shard_map/ppermute | solution.py:423
  22.2 15.5 %collective-permute-start.10 = (bf16[512,128]{1,0:T(8,128)(2,1)}, bf16[512,128]{1,0:T(8,128)(2,1)S(1)}, u32[]{:S(2)}, u32[]{:S(2)}) collective-permute-start(bf16[512,128]{1,0:T(8,128)(2,1)} %get-tuple-element.7.refs_4_), channel_id=1, source_target_pairs={{0,8},{4,12},{8,0},{12,4},{1,9},{5,13},{9,1},{13,5},{2,10},{6,14},... | collective-permute-start | bytes 393224 | tf_op jit(solution)/shard_map/ppermute | solution.py:423
  23.9 13.8 %collective-permute-start.9 = (bf16[512,128]{1,0:T(8,128)(2,1)}, bf16[512,128]{1,0:T(8,128)(2,1)S(1)}, u32[]{:S(2)}, u32[]{:S(2)}) collective-permute-start(bf16[512,128]{1,0:T(8,128)(2,1)} %get-tuple-element.7.refs_4_), channel_id=1, source_target_pairs={{0,4},{4,0},{8,12},{12,8},{1,5},{5,1},{9,13},{13,9},{2,6},{6,2},{1... | collective-permute-start | bytes 393224 | tf_op jit(solution)/shard_map/ppermute | solution.py:423
  25.3 6.6 %collective-permute-start.5 = (bf16[512,128]{1,0:T(8,128)(2,1)}, bf16[512,128]{1,0:T(8,128)(2,1)S(1)}, u32[]{:S(2)}, u32[]{:S(2)}) collective-permute-start(bf16[512,128]{1,0:T(8,128)(2,1)} %get-tuple-element.6), channel_id=1, source_target_pairs={{0,2},{2,0},{1,3},{3,1},{4,6},{6,4},{5,7},{7,5},{8,10},{10,8},{9,1... | collective-permute-start | bytes 393224 | tf_op jit(solution)/shard_map/ppermute | solution.py:423
  26.7 63.2 %collective-permute-start = (bf16[16,128,256]{2,1,0:T(8,128)(2,1)}, bf16[16,128,256]{2,1,0:T(8,128)(2,1)S(1)}, u32[]{:S(2)}, u32[]{:S(2)}) collective-permute-start(bf16[16,128,256]{2,1,0:T(8,128)(2,1)} %get-tuple-element.5.own_ref), channel_id=1, source_target_pairs={{0,2},{2,0},{1,3},{3,1},{4,6},{6,4},{5,7},{7,5},{8,10},{10,8},{9,1... | collective-permute-start | bytes 3145736 | tf_op jit(solution)/shard_map/ppermute | solution.py:423
  28.2 61.7 %copy-start.1 = (bf16[8,64,128]{2,1,0:T(8,128)(2,1)}, bf16[8,64,128]{2,1,0:T(8,128)(2,1)S(1)}, u32[]{:S(2)}) copy-start(bf16[8,64,128]{2,1,0:T(8,128)(2,1)S(1)} %get-tuple-element.15.b00) | copy-start | bytes 393220
  31.8 23.0 %collective-permute-start.2 = (bf16[8,64,128]{2,1,0:T(8,128)(2,1)S(1)}, bf16[8,64,128]{2,1,0:T(8,128)(2,1)S(1)}, u32[]{:S(2)}, u32[]{:S(2)}) collective-permute-start(bf16[8,64,128]{2,1,0:T(8,128)(2,1)S(1)} %get-tuple-element.14), channel_id=1, source_target_pairs={{0,2},{2,0},{1,3},{3,1},{4,6},{6,4},{5,7},{7,5},{8,10},{10,8},{9,1... | collective-permute-start | bytes 393224 | tf_op jit(solution)/shard_map/ppermute | solution.py:423
  34.9 20.6 %copy-start.5 = (bf16[512,128]{1,0:T(8,128)(2,1)}, bf16[512,128]{1,0:T(8,128)(2,1)S(1)}, u32[]{:S(2)}) copy-start(bf16[512,128]{1,0:T(8,128)(2,1)S(1)} %collective-permute-done.11.refs_7_) | copy-start | bytes 393220
  34.9 6.7 %collective-permute-start.8 = (bf16[256,128]{1,0:T(8,128)(2,1)S(1)}, bf16[256,128]{1,0:T(8,128)(2,1)S(1)}, u32[]{:S(2)}, u32[]{:S(2)}) collective-permute-start(bf16[256,128]{1,0:T(8,128)(2,1)S(1)} %get-tuple-element.8), channel_id=1, source_target_pairs={{0,12},{4,8},{8,4},{12,0},{1,13},{5,9},{9,5},{13,1},{2,14},{6,10},... | collective-permute-start | bytes 196616 | tf_op jit(solution)/shard_map/ppermute | solution.py:423
  37.7 17.9 %copy-start.6 = (bf16[512,128]{1,0:T(8,128)(2,1)}, bf16[512,128]{1,0:T(8,128)(2,1)S(1)}, u32[]{:S(2)}) copy-start(bf16[512,128]{1,0:T(8,128)(2,1)S(1)} %collective-permute-done.10.refs_6_) | copy-start | bytes 393220
  37.7 17.9 %collective-permute-start.7 = (bf16[256,128]{1,0:T(8,128)(2,1)S(1)}, bf16[256,128]{1,0:T(8,128)(2,1)S(1)}, u32[]{:S(2)}, u32[]{:S(2)}) collective-permute-start(bf16[256,128]{1,0:T(8,128)(2,1)S(1)} %get-tuple-element.9), channel_id=1, source_target_pairs={{0,8},{4,12},{8,0},{12,4},{1,9},{5,13},{9,1},{13,5},{2,10},{6,14},... | collective-permute-start | bytes 196616 | tf_op jit(solution)/shard_map/ppermute | solution.py:423
  37.7 17.9 %copy-start.7 = (bf16[512,128]{1,0:T(8,128)(2,1)}, bf16[512,128]{1,0:T(8,128)(2,1)S(1)}, u32[]{:S(2)}) copy-start(bf16[512,128]{1,0:T(8,128)(2,1)S(1)} %collective-permute-done.9.refs_5_) | copy-start | bytes 393220
  37.7 17.8 %collective-permute-start.6 = (bf16[256,128]{1,0:T(8,128)(2,1)S(1)}, bf16[256,128]{1,0:T(8,128)(2,1)S(1)}, u32[]{:S(2)}, u32[]{:S(2)}) collective-permute-start(bf16[256,128]{1,0:T(8,128)(2,1)S(1)} %get-tuple-element.10), channel_id=1, source_target_pairs={{0,4},{4,0},{8,12},{12,8},{1,5},{5,1},{9,13},{13,9},{2,6},{6,2},{1... | collective-permute-start | bytes 196616 | tf_op jit(solution)/shard_map/ppermute | solution.py:423
  41.6 14.0 %copy-start.11 = (bf16[256,128]{1,0:T(8,128)(2,1)}, bf16[256,128]{1,0:T(8,128)(2,1)S(1)}, u32[]{:S(2)}) copy-start(bf16[256,128]{1,0:T(8,128)(2,1)S(1)} %collective-permute-done.8.refs_3_) | copy-start | bytes 196612
  41.6 48.4 %collective-permute-start.3 = (bf16[8,64,128]{2,1,0:T(8,128)(2,1)S(1)}, bf16[8,64,128]{2,1,0:T(8,128)(2,1)S(1)}, u32[]{:S(2)}, u32[]{:S(2)}) collective-permute-start(bf16[8,64,128]{2,1,0:T(8,128)(2,1)S(1)} %get-tuple-element.15.b00), channel_id=1, source_target_pairs={{0,4},{4,0},{8,12},{12,8},{1,5},{5,1},{9,13},{13,9},{2,6},{6,2},{1... | collective-permute-start | bytes 393224 | tf_op jit(solution)/shard_map/ppermute | solution.py:423
  54.9 35.1 %copy-start.8 = (bf16[8,64,128]{2,1,0:T(8,128)(2,1)}, bf16[8,64,128]{2,1,0:T(8,128)(2,1)S(1)}, u32[]{:S(2)}) copy-start(bf16[8,64,128]{2,1,0:T(8,128)(2,1)S(1)} %collective-permute-done.2.b01) | copy-start | bytes 393220
  54.9 35.1 %collective-permute-start.4 = (bf16[8,64,128]{2,1,0:T(8,128)(2,1)S(1)}, bf16[8,64,128]{2,1,0:T(8,128)(2,1)S(1)}, u32[]{:S(2)}, u32[]{:S(2)}) collective-permute-start(bf16[8,64,128]{2,1,0:T(8,128)(2,1)S(1)} %collective-permute-done.2.b01), channel_id=1, source_target_pairs={{0,4},{4,0},{8,12},{12,8},{1,5},{5,1},{9,13},{13,9},{2,6},{6,2},{1... | collective-permute-start | bytes 393224 | tf_op jit(solution)/shard_map/ppermute | solution.py:423
  55.5 0.6 copy-start.12
  55.5 0.6 copy-start.13
  90.0 0.6 copy-start.9
  90.0 0.7 copy-start.10
  90.0 1.0 copy-start.4

commit v2 on v1

v2 whole, which is shorter than its diff:
```python
import functools

import jax
import jax.numpy as jnp
from jax import lax
from jax.experimental import pallas as pl
from jax.experimental.pallas import tpu as pltpu
from jax.sharding import PartitionSpec as P


EPS = 1e-05
LANES = 128
LOG2E = 1.4426950408889634


def standardize_features(x, gain):
    mean = jnp.mean(x, axis=-1, keepdims=True)
    var = jnp.mean((x - mean) ** 2, axis=-1, keepdims=True)
    return (x - mean) * lax.rsqrt(var + EPS) * gain


def gathered(
    alignment_tensor,
    residue_grid,
    mixing_scale_vector,
    logit_offset_scale,
    feedforward_scale,
    product_scale_vector,
    grid_scale_vector,
    logit_offset_map,
    asking_mapping,
    lookup_mapping,
    content_mapping,
    mixing_return_matrix,
    alignment_widen_map,
    alignment_shrink_map,
    former_embedding_map,
    latter_embedding_map,
    product_return_map,
    grid_widen_map,
    grid_shrink_map,
):
    sample_alignment = alignment_tensor[0]
    local_pair = residue_grid[0]
    subspace_total = logit_offset_map.shape[1]
    feature_extent = sample_alignment.shape[-1]
    subspace_number = feature_extent // subspace_total
    sequences_available = sample_alignment.shape[0]
    chain_available = sample_alignment.shape[1]
    tile_rows = local_pair.shape[0]
    tile_cols = local_pair.shape[1]
    product_extent = former_embedding_map.shape[1]
    product_operands = standardize_features(sample_alignment, product_scale_vector).astype(
        jnp.bfloat16
    )
    former_tensor = jnp.dot(
        product_operands, former_embedding_map, preferred_element_type=jnp.float32
    ).astype(jnp.bfloat16)
    latter_tensor = jnp.dot(
        product_operands, latter_embedding_map, preferred_element_type=jnp.float32
    ).astype(jnp.bfloat16)
    left_rows, right_rows = (
        lax.all_gather(former_tensor, "tile", axis=0, tiled=True),
        lax.all_gather(latter_tensor, "tile", axis=0, tiled=True),
    )
    left_all = lax.all_gather(left_rows, "col", axis=1, tiled=True)
    left_mine = lax.dynamic_slice_in_dim(left_all, lax.axis_index("tile") * tile_rows, tile_rows, 1)
    tensor_product = (
        jnp.einsum("era,eyq->ryaq", left_mine, right_rows, preferred_element_type=jnp.float32)
        / left_rows.shape[0]
    )
    update = jnp.dot(
        tensor_product.reshape(tile_rows, tile_cols, product_extent * product_extent),
        product_return_map,
        precision=lax.Precision.HIGHEST,
    )
    bias_tile = jnp.einsum(
        "ijc,ch->hij",
        standardize_features(local_pair, logit_offset_scale),
        logit_offset_map,
        precision=lax.Precision.HIGHEST,
    )
    wide = lax.all_gather(bias_tile, "col", axis=2, tiled=True)
    whole = lax.all_gather(wide.astype(jnp.bfloat16), "tile", axis=1, tiled=True).astype(wide.dtype)
    bias = lax.dynamic_slice_in_dim(
        whole, lax.axis_index("col") * chain_available, chain_available, 1
    )
    standardized_source = standardize_features(sample_alignment, mixing_scale_vector).astype(
        jnp.bfloat16
    )
    asking_vectors = jnp.dot(
        standardized_source, asking_mapping, preferred_element_type=jnp.float32
    ).astype(jnp.bfloat16)
    lookup_vectors = jnp.dot(
        standardized_source, lookup_mapping, preferred_element_type=jnp.float32
    ).astype(jnp.bfloat16)
    content_vectors = jnp.dot(
        standardized_source, content_mapping, preferred_element_type=jnp.float32
    ).astype(jnp.bfloat16)
    all_keys, all_values = (
        lax.all_gather(lookup_vectors, "col", axis=1, tiled=True),
        lax.all_gather(content_vectors, "col", axis=1, tiled=True),
    )
    total_res = all_keys.shape[1]
    asking_vectors = asking_vectors.reshape(
        sequences_available, chain_available, subspace_total, subspace_number
    )
    all_keys = all_keys.reshape(sequences_available, total_res, subspace_total, subspace_number)
    all_values = all_values.reshape(sequences_available, total_res, subspace_total, subspace_number)
    scores = (
        jnp.einsum("sqhd,skhd->shqk", asking_vectors, all_keys, preferred_element_type=jnp.float32)
        / jnp.sqrt(jnp.float32(subspace_number))
        + bias[None]
    )
    weights = jax.nn.softmax(scores, axis=-1).astype(jnp.bfloat16)
    mixing_outcome = jnp.einsum(
        "shqk,skhd->sqhd", weights, all_values, preferred_element_type=jnp.float32
    )
    mixing_outcome = mixing_outcome.astype(jnp.bfloat16).reshape(
        sequences_available, chain_available, feature_extent
    )
    alignment_activations = sample_alignment + jnp.dot(
        mixing_outcome, mixing_return_matrix, preferred_element_type=jnp.float32
    )
    expanded_features = jax.nn.relu(
        jnp.dot(
            standardize_features(alignment_activations, feedforward_scale).astype(jnp.bfloat16),
            alignment_widen_map,
            preferred_element_type=jnp.float32,
        )
    ).astype(jnp.bfloat16)
    alignment_revised = alignment_activations + jnp.dot(
        expanded_features, alignment_shrink_map, preferred_element_type=jnp.float32
    )
    pair_mid = local_pair + update
    spread = jax.nn.relu(
        jnp.dot(
            standardize_features(pair_mid, grid_scale_vector).astype(jnp.bfloat16),
            grid_widen_map,
            preferred_element_type=jnp.float32,
        )
    ).astype(jnp.bfloat16)
    grid_revised = pair_mid + jnp.dot(spread, grid_shrink_map, preferred_element_type=jnp.float32)
    return (alignment_revised[None], grid_revised[None])


def normalized(x):
    mean = jnp.mean(x, axis=-1, keepdims=True)
    centered = x - mean
    var = jnp.mean(centered * centered, axis=-1, keepdims=True)
    return centered * lax.rsqrt(var + EPS)


def normalized_down(x):
    mean = jnp.mean(x, axis=0, keepdims=True)
    centered = x - mean
    var = jnp.mean(centered * centered, axis=0, keepdims=True)
    return centered * lax.rsqrt(var + EPS)


def down(row):
    return jnp.broadcast_to(row, (8, row.shape[1])).T[:, :1]


def dot(a, b, dims=((1,), (0,))):
    return lax.dot_general(a, b, (dims, ((), ())), preferred_element_type=jnp.float32)


def factors_kernel(rows, upper, x_ref, mix_ref, gain_ref, wl_ref, wr_ref, normed_ref, even_ref, odd_ref, right_ref, std, half_scaled, lacc, racc):
    step = pl.program_id(0)
    block, residues, features = x_ref.shape
    extent = wl_ref.shape[0]
    pack = LANES // extent
    groups = residues // pack
    spans = features // LANES
    source = lax.broadcasted_iota(jnp.int32, (extent, LANES), 0)
    target = lax.broadcasted_iota(jnp.int32, (extent, LANES), 1)
    wides = []
    for a in range(pack):
        spread = (source + a * extent == target).astype(jnp.bfloat16)
        wides.append(dot(wl_ref[...], spread, ((0,), (0,))).astype(jnp.bfloat16))
    for t in range(block + 1):
        if t < block:
            base = normalized(x_ref[t])
            normed_ref[t] = (base * mix_ref[...]).astype(jnp.bfloat16)
            scaled = base * gain_ref[...]
            for f in range(spans):
                std[t, f] = scaled[:, f * LANES : (f + 1) * LANES]
            half_scaled[t] = scaled.astype(jnp.bfloat16)
        if t >= 1:
            k = t - 1
            row = step * block + k
            racc[pl.ds(row, extent, stride=rows), :] = dot(wr_ref[...], half_scaled[k], ((1,), (1,)))
            packed = jnp.zeros((groups, LANES), jnp.float32)
            for a in range(pack):
                picked = [std[k, f, pl.ds(a, groups, stride=pack), :] for f in range(spans)]
                packed = packed + dot(jnp.concatenate(picked, axis=1).astype(jnp.bfloat16), wides[a])
            lacc[pl.ds(row, groups, stride=rows), :] = packed

    @pl.when(step == pl.num_programs(0) - 1)
    def _():
        size = even_ref.shape[0]
        at = lax.axis_index("tile") % upper
        for mask, ref in enumerate((even_ref, odd_ref)):
            ref[...] = lacc[pl.ds(pl.multiple_of((at ^ mask) * size, size), size), :].astype(jnp.bfloat16)
        right_ref[...] = racc[...].astype(jnp.bfloat16)


def factors(x, mix, gain, wl, wr, upper, block):
    rows, residues, features = x.shape
    extent = wl.shape[0]
    groups = residues * extent // LANES
    whole = lambda shape: pl.BlockSpec(shape, lambda i: (0,) * len(shape))
    tile = pl.BlockSpec((block, residues, features), lambda i: (i, 0, 0))
    return pl.pallas_call(
        functools.partial(factors_kernel, rows, upper),
        grid=(rows // block,),
        in_specs=[tile, whole((1, features)), whole((1, features)), whole(wl.shape), whole(wr.shape)],
        out_specs=[tile, *[whole((groups * rows // upper, LANES))] * 2, whole((extent * rows, residues))],
        out_shape=[
            jax.ShapeDtypeStruct((rows, residues, features), jnp.bfloat16),
            *[jax.ShapeDtypeStruct((groups * rows // upper, LANES), jnp.bfloat16)] * 2,
            jax.ShapeDtypeStruct((extent * rows, residues), jnp.bfloat16),
        ],
        scratch_shapes=[
            pltpu.VMEM((block, features // LANES, residues, LANES), jnp.float32),
            pltpu.VMEM((block, residues, features), jnp.bfloat16),
            pltpu.VMEM((groups * rows, LANES), jnp.float32),
            pltpu.VMEM((extent * rows, residues), jnp.float32),
        ],
        name="factors",
        cost_estimate=pl.CostEstimate(
            flops=2 * rows * residues * features * 5 * extent,
            bytes_accessed=rows * residues * features * 6,
            transcendentals=rows * residues,
        ),
    )(x, mix.reshape(1, -1), gain.reshape(1, -1), wl, wr)


def bias_kernel(heads, x_ref, gain_ref, w_ref, out_ref, acc):
    step = pl.program_id(0)
    block, _, _ = x_ref.shape
    rows = acc.shape[0] // heads
    w = w_ref[...].astype(jnp.bfloat16)
    gain = down(gain_ref[...])
    turned, scaled = {}, {}
    for t in range(block + 2):
        if t >= 2:
            acc[pl.ds(step * block + t - 2, heads, stride=rows), :] = dot(w, scaled.pop(t - 2))
        if t < block:
            turned[t] = x_ref[t].T
        if 1 <= t <= block:
            scaled[t - 1] = (normalized_down(turned.pop(t - 1)) * gain).astype(jnp.bfloat16)

    @pl.when(step == pl.num_programs(0) - 1)
    def _():
        out_ref[...] = acc[...].astype(jnp.bfloat16)


def pair_bias(pair, gain, w, block):
    rows, cols, features = pair.shape
    heads = w.shape[0]
    whole = lambda shape: pl.BlockSpec(shape, lambda i: (0,) * len(shape))
    return pl.pallas_call(
        functools.partial(bias_kernel, heads),
        grid=(rows // block,),
        in_specs=[
            pl.BlockSpec((block, cols, features), lambda i: (i, 0, 0)),
            whole((1, features)),
            whole(w.shape),
        ],
        out_specs=whole((heads * rows, cols)),
        out_shape=jax.ShapeDtypeStruct((heads * rows, cols), jnp.bfloat16),
        scratch_shapes=[pltpu.VMEM((heads * rows, cols), jnp.float32)],
        name="pair_bias",
        cost_estimate=pl.CostEstimate(
            flops=2 * rows * cols * features * heads * 8,
            bytes_accessed=rows * cols * features * 4,
            transcendentals=rows * cols,
        ),
    )(pair, gain.reshape(1, -1), w).reshape(heads, rows, cols)


def pair_kernel(masks, upper, rows, extent, *refs):
    parts = len(masks)
    lefts, rights = refs[:parts], refs[parts : 2 * parts]
    pair_ref, map_ref, gain_ref, wide_ref, shrink_ref, out_ref = refs[2 * parts : 2 * parts + 6]
    rall, lall, outer, maps, wt, wide_t, shrink_t, gains, middle, normed, hidden = refs[2 * parts + 6 :]
    step = pl.program_id(0)
    last = pl.num_programs(0) - 1
    block, cols, _ = pair_ref.shape
    bf16 = jnp.bfloat16

    @pl.when(step == 0)
    def _():
        tile = lax.axis_index("tile")
        crossed = (tile // upper != lax.axis_index("col")).astype(jnp.int32) * upper
        for mask, right in zip(masks, rights):
            start = pl.multiple_of((crossed ^ mask) * rows, rows)
            for d in range(extent):
                rall[pl.ds(start, rows), d * cols : (d + 1) * cols] = right[d * rows : (d + 1) * rows, :]
        for r in range(lefts[0].shape[0] // rows):
            stacked = jnp.concatenate([left[r * rows : (r + 1) * rows, :] for left in lefts], axis=0)
            lall[r * LANES : (r + 1) * LANES, :] = stacked.T
        for d in range(extent):
            picked = map_ref[pl.ds(d, extent, stride=extent), :] * (1.0 / (parts * rows))
            maps[d * extent : (d + 1) * extent, :] = picked
        wt[...] = maps[...].T.astype(bf16)
        wide_t[...] = wide_ref[...].T
        shrink_t[...] = shrink_ref[...].T
        gains[...] = jnp.broadcast_to(down(gain_ref[...]), gains.shape)

    fresh, ready = step % 2, (step + 1) % 2
    duo = 2
    size = block * extent
    first = pl.multiple_of(jnp.minimum(step, last - 1) * size, size)

    heights = 2 if block % 4 == 0 else 1
    height = block // heights

    def product(n):
        c, v = n // heights, n % heights
        lanes = slice(c * duo * cols, (c + 1) * duo * cols)
        start = pl.multiple_of(first + v * height * extent, height * extent)
        made = dot(lall[pl.ds(start, height * extent), :], rall[:, lanes]).astype(bf16)
        for i in range(height):
            row = v * height + i
            for d in range(duo):
                at = (c * duo + d) * extent
                outer[fresh, row // 2, at : at + extent, row % 2 * cols : (row % 2 + 1) * cols] = made[
                    i * extent : (i + 1) * extent, d * cols : (d + 1) * cols
                ]

    def update(k):
        mid = dot(wt[...], outer[ready, k])
        middle[k] = mid + jnp.concatenate([pair_ref[2 * k].T, pair_ref[2 * k + 1].T], axis=1)

    def scale(k):
        normed[k] = (normalized_down(middle[k]) * gains[...]).astype(bf16)

    split = hidden.shape[1] // 2

    def widen(c, k):
        at = slice(c * split, (c + 1) * split)
        hidden[k, at, :] = jnp.maximum(dot(wide_t[at, :], normed[k]), 0.0).astype(bf16)

    def shrink(k):
        done = middle[k] + dot(shrink_t[...], hidden[k])
        for i in range(2):
            out_ref[2 * k + i] = done[:, i * cols : (i + 1) * cols].T

    pairs = block // 2
    stages = (
        (0, update),
        (1, scale),
        (2, functools.partial(widen, 0)),
        (2, functools.partial(widen, 1)),
        (3, shrink),
    )
    feed = []
    for t in range(pairs + 3):
        for lag, stage in stages:
            if 0 <= t - lag < pairs:
                feed.append(functools.partial(stage, t - lag))
    chunks = extent // duo * heights

    @pl.when(step == 0)
    def _():
        for c in range(chunks):
            product(c)

    @pl.when((step > 0) & (step < last))
    def _():
        for n, piece in enumerate(feed):
            for c in range(n * chunks // len(feed), (n + 1) * chunks // len(feed)):
                product(c)
            piece()

    @pl.when(step == last)
    def _():
        for piece in feed:
            piece()


def pair_update(lefts, rights, masks, upper, pair, maps, gain, wide, shrink, rows, block):
    parts = len(lefts)
    tile_rows, cols, channels = pair.shape
    extent = rights[0].shape[0] // rows
    pairs = block // 2
    whole = lambda shape: pl.BlockSpec(shape, lambda i: (0,) * len(shape))
    tile = pl.BlockSpec((block, cols, channels), lambda i: (jnp.maximum(i - 1, 0), 0, 0))
    return pl.pallas_call(
        functools.partial(pair_kernel, masks, upper, rows, extent),
        grid=(tile_rows // block + 1,),
        in_specs=[whole(a.shape) for a in (*lefts, *rights)]
        + [tile, whole(maps.shape), whole((1, channels)), whole(wide.shape), whole(shrink.shape)],
        out_specs=tile,
        out_shape=jax.ShapeDtypeStruct(pair.shape, jnp.float32),
        scratch_shapes=[
            pltpu.VMEM((parts * rows, extent * cols), jnp.bfloat16),
            pltpu.VMEM((tile_rows * extent, parts * rows), jnp.bfloat16),
            pltpu.VMEM((2, pairs, extent * extent, 2 * cols), jnp.bfloat16),
            pltpu.VMEM((extent * extent, channels), jnp.float32),
            pltpu.VMEM((channels, extent * extent), jnp.bfloat16),
            pltpu.VMEM(wide.shape[::-1], jnp.bfloat16),
            pltpu.VMEM(shrink.shape[::-1], jnp.bfloat16),
            pltpu.VMEM((channels, 2 * cols), jnp.float32),
            pltpu.VMEM((pairs, channels, 2 * cols), jnp.float32),
            pltpu.VMEM((pairs, channels, 2 * cols), jnp.bfloat16),
            pltpu.VMEM((pairs, wide.shape[1], 2 * cols), jnp.bfloat16),
        ],
        name="pair_update",
        cost_estimate=pl.CostEstimate(
            flops=2 * tile_rows * cols * (extent * extent * (parts * rows + channels) + 2 * wide.size) * 2,
            bytes_accessed=pair.size * 8,
            transcendentals=tile_rows * cols,
        ),
    )(*lefts, *rights, pair, maps, gain.reshape(1, -1), wide, shrink)


def attention_kernel(
    heads, cols, x_ref, own_ref, far_ref, b0, b1, b2, b3, wq_ref, wk_ref, wv_ref, wo_ref, gain_ref, wide_ref,
    shrink_ref, out_ref, bias, natural, wq, wv, wo, wide_t, shrink_t, gains, masked, keys, values, score, weight,
    attended, middle, normed, hidden,
):
    step = pl.program_id(0)
    block, residues, features = x_ref.shape
    depth = features // heads
    half = residues // 2
    bf16 = jnp.bfloat16
    group = LANES // depth
    pairs = heads // 2
    units = block * pairs
    sides = features // LANES

    @pl.when(step == 0)
    def _():
        for h in range(heads):
            for r, tile in enumerate((b0, b1, b2, b3)):
                source = lax.axis_index("tile") ^ r
                top = pl.multiple_of(source // cols * half, half)
                edge = pl.multiple_of((source % cols ^ lax.axis_index("col")) * residues, residues)
                natural[pl.ds(top, half), pl.ds(edge, residues)] = tile[h].astype(jnp.float32) * LOG2E
            for side in range(2):
                bias[h // 2, side * residues : (side + 1) * residues, (h % 2) * residues : (h % 2 + 1) * residues] = (
                    natural[:, side * residues : (side + 1) * residues].T
                )
        for turned, ref in ((wq, wq_ref), (wv, wv_ref), (wo, wo_ref), (wide_t, wide_ref), (shrink_t, shrink_ref)):
            turned[...] = ref[...].T
        gains[...] = jnp.broadcast_to(down(gain_ref[...]), gains.shape)
        masked[...] = jnp.zeros_like(masked)
        for u in range(units):
            values[u, 2 * depth :, :] = jnp.ones((16, 2 * residues), bf16)

    def project():
        factor = LOG2E / (depth**0.5)
        own = own_ref[...].reshape(block * residues, features)
        far = far_ref[...].reshape(block * residues, features)
        query = (dot(wq[...], own, ((1,), (1,))) * factor).astype(bf16)
        for s in range(block):
            for h in range(heads):
                masked[
                    s * pairs + h // 2, h % group * depth : (h % group + 1) * depth, h % 2 * residues : (h % 2 + 1) * residues
                ] = query[h * depth : (h + 1) * depth, s * residues : (s + 1) * residues]
        for side, rows in enumerate((own, far)):
            key = dot(rows, wk_ref[...]).astype(bf16)
            value = dot(wv[...], rows, ((1,), (1,))).astype(bf16)
            for s in range(block):
                at = slice(s * residues, (s + 1) * residues)
                for f in range(sides):
                    keys[s, f, side * residues : (side + 1) * residues, :] = key[at, f * LANES : (f + 1) * LANES]
                for g in range(pairs):
                    values[s * pairs + g, : 2 * depth, side * residues : (side + 1) * residues] = value[
                        2 * g * depth : 2 * (g + 1) * depth, at
                    ]

    def stand():
        mid = x_ref[...].reshape(block * residues, features).T + dot(wo[...], attended[...])
        middle[...] = mid
        normed[...] = (normalized_down(mid) * gains[...]).astype(bf16)

    widths = 16
    chunk = hidden.shape[0] // widths
    part = features // 2

    def widen(c):
        at = slice(c * chunk, (c + 1) * chunk)
        hidden[at, :] = jnp.maximum(dot(wide_t[at, :], normed[...]), 0.0).astype(bf16)

    def shrink(c):
        at = slice(c * part, (c + 1) * part)
        done = middle[at, :] + dot(shrink_t[at, :], hidden[...])
        out_ref[:, :, at] = done.T.reshape(block, residues, part)

    feed = [functools.partial(widen, c) for c in range(widths)] + [functools.partial(shrink, c) for c in range(2)]

    def scores(u, i):
        s, g = u // pairs, u % pairs
        at = slice(i * residues, (i + 1) * residues)
        score[u % 2, at, :] = dot(keys[s, 2 * g // group, at, :], masked[u]) + bias[g, at, :]

    def soften(u, i):
        lanes = slice(i * residues, (i + 1) * residues)
        now = score[u % 2, :, lanes]
        weight[u % 2, :, lanes] = jnp.exp2(now - jnp.max(now, axis=0, keepdims=True)).astype(bf16)

    def attend(u):
        s, g = u // pairs, u % pairs
        out = dot(values[u], weight[u % 2])
        norm = 1.0 / out[2 * depth : 2 * depth + 1, :]
        for i in range(2):
            lanes = slice(i * residues, (i + 1) * residues)
            attended[(2 * g + i) * depth : (2 * g + i + 1) * depth, s * residues : (s + 1) * residues] = (
                out[i * depth : (i + 1) * depth, lanes] * norm[:, lanes]
            ).astype(bf16)

    def mix(left):
        for t in range(units + 2):
            for i in range(2):
                if i == 0 and t >= 2:
                    attend(t - 2)
                if t < units:
                    scores(t, i)
                if left:
                    left.pop(0)()
                if 1 <= t <= units:
                    soften(t - 1, i)

    @pl.when(step == 0)
    def _():
        project()
        mix([])

    @pl.when((step > 0) & (step < pl.num_programs(0) - 1))
    def _():
        stand()
        project()
        mix(list(feed))

    @pl.when(step == pl.num_programs(0) - 1)
    def _():
        stand()
        for piece in feed:
            piece()


def attention(cols, x, own, far, biases, weights, gain, wide, shrink, block):
    rows, residues, features = x.shape
    heads = biases[0].shape[0]
    depth = features // heads
    units = block * heads // 2
    steps = rows // block
    wide_residues = 2 * residues
    whole = lambda shape: pl.BlockSpec(shape, lambda i: (0,) * len(shape))
    tile = pl.BlockSpec((block, residues, features), lambda i: (jnp.minimum(i, steps - 1), 0, 0))
    late = pl.BlockSpec((block, residues, features), lambda i: (jnp.maximum(i - 1, 0), 0, 0))
    return pl.pallas_call(
        functools.partial(attention_kernel, heads, cols),
        grid=(steps + 1,),
        in_specs=[late, tile, tile]
        + [whole(b.shape) for b in biases]
        + [whole(w.shape) for w in weights]
        + [whole((1, features)), whole(wide.shape), whole(shrink.shape)],
        out_specs=late,
        scratch_shapes=[
            pltpu.VMEM((heads // 2, wide_residues, wide_residues), jnp.float32),
            pltpu.VMEM((residues, wide_residues), jnp.float32),
            *[pltpu.VMEM((features, features), jnp.bfloat16)] * 3,
            pltpu.VMEM(wide.shape[::-1], jnp.bfloat16),
            pltpu.VMEM(shrink.shape[::-1], jnp.bfloat16),
            pltpu.VMEM((features, block * residues), jnp.float32),
            pltpu.VMEM((units, LANES, wide_residues), jnp.bfloat16),
            pltpu.VMEM((block, features // LANES, wide_residues, LANES), jnp.bfloat16),
            pltpu.VMEM((units, 2 * depth + 16, wide_residues), jnp.bfloat16),
            pltpu.VMEM((2, wide_residues, wide_residues), jnp.float32),
            pltpu.VMEM((2, wide_residues, wide_residues), jnp.bfloat16),
            pltpu.VMEM((features, block * residues), jnp.bfloat16),
            pltpu.VMEM((features, block * residues), jnp.float32),
            pltpu.VMEM((features, block * residues), jnp.bfloat16),
            pltpu.VMEM((wide.shape[1], block * residues), jnp.bfloat16),
        ],
        out_shape=jax.ShapeDtypeStruct(x.shape, jnp.float32),
        name="attention",
        cost_estimate=pl.CostEstimate(
            flops=2 * rows * residues * (6 * features * features + 4 * heads * residues * features + 2 * wide.size),
            bytes_accessed=rows * residues * features * 12,
            transcendentals=rows * residues * heads * 2 * residues,
        ),
    )(x, own, far, *biases, *weights, gain.reshape(1, -1), wide, shrink)


def exchanged(
    alignment_tensor,
    residue_grid,
    mixing_scale_vector,
    logit_offset_scale,
    feedforward_scale,
    product_scale_vector,
    grid_scale_vector,
    logit_offset_map,
    asking_mapping,
    lookup_mapping,
    content_mapping,
    mixing_return_matrix,
    alignment_widen_map,
    alignment_shrink_map,
    former_embedding_map,
    latter_embedding_map,
    product_return_map,
    grid_widen_map,
    grid_shrink_map,
):
    msa, pair = alignment_tensor[0], residue_grid[0]
    rows = msa.shape[0]
    tiles = lax.axis_size("tile")
    upper = tiles // 2

    def swap(value, axis, mask):
        return lax.ppermute(value, axis, [(i, i ^ mask) for i in range(lax.axis_size(axis))])

    cols = lax.axis_size("col")
    normed, even, odd, right = factors(
        msa,
        mixing_scale_vector,
        product_scale_vector,
        former_embedding_map.T,
        latter_embedding_map.T,
        upper,
        min(rows, 8),
    )
    devices = [(t, c) for t in range(tiles) for c in range(cols)]

    def route(value, goal):
        pairs = [(t * cols + c, goal(t, c)[0] * cols + goal(t, c)[1]) for t, c in devices]
        return lax.ppermute(value, ("tile", "col"), pairs)

    def owner(r):
        def goal(t, c):
            aim = t ^ r
            return (aim, c) if aim // upper == c else (aim ^ upper, 1 - c)

        return goal

    right_up = swap(right, "tile", upper)
    lefts = []
    for r in range(tiles):
        lefts.append(route(odd if r % upper else even, owner(r)))
    right_side = swap(right, "tile", 1)
    normed_far = swap(normed, "col", 1)

    pair, _ = lax.optimization_barrier((pair, right))
    tile_bias = pair_bias(pair, logit_offset_scale, logit_offset_map.T, min(pair.shape[0], 32))
    tile_bias, right_up = lax.optimization_barrier((tile_bias, right_up))
    rights = [right, right_up, right_side, swap(right_up, "tile", 1)]
    masks = (0, upper, 1, upper + 1)
    biases = [
        route(tile_bias, lambda t, c, r=r: ((t % upper * cols + c) ^ r, t // upper)) for r in range(tiles)
    ]

    grid_revised = pair_update(
        lefts, rights, masks, upper, pair, product_return_map, grid_scale_vector, grid_widen_map, grid_shrink_map, rows, 16
    )
    alignment_revised = attention(
        cols,
        msa,
        normed,
        normed_far,
        biases,
        (asking_mapping, lookup_mapping, content_mapping, mixing_return_matrix),
        feedforward_scale,
        alignment_widen_map,
        alignment_shrink_map,
        2,
    )
    return (alignment_revised[None], grid_revised[None])


def on_device(*args):
    msa, pair = args[0], args[1]
    extent = args[14].shape[1]
    fits = (
        lax.axis_size("col") == 2
        and lax.axis_size("tile") == 4
        and msa.shape[1] % 16 == 0
        and msa.shape[2] == LANES
        and pair.shape[1] % 16 == 0
        and pair.shape[2] == LANES
        and LANES % extent == 0
        and extent % 16 == 0
    )
    if not fits:
        return gathered(*args)
    return exchanged(*args)


def solution(mesh):
    placed = (
        P(("groups", "branch"), "tile", "col", None),
        P(("groups", "branch"), "tile", "col", None),
        P(),
        P(),
        P(),
        P(),
        P(),
        P(),
        P(),
        P(),
        P(),
        P(),
        P(),
        P(),
        P(),
        P(),
        P(),
        P(),
        P(),
    )
    return jax.shard_map(
        on_device,
        mesh=mesh,
        in_specs=placed,
        out_specs=(
            P(("groups", "branch"), "tile", "col", None),
            P(("groups", "branch"), "tile", "col", None),
        ),
        check_vma=False,
    )
```

time: 137 us -> 77.3 us (0.56)
  Pallas kernels: 92.3 us -> 44 us
  waiting for transfers between devices: 19.5 us -> 2.99 us
  starting transfers between devices: 15.6 us -> 28.2 us
  local copies, waits for them, and re-layouts: 6.12 us -> 1.05 us
  other arithmetic: 1.9 us -> 0 us
    pallas_call x3, Pallas kernels: 84.7 us -> 39.7 us  [the longest x1 17.7 us: attention(): pl.pallas_call(functools.partial(attention_kernel, heads, cols), grid=(st...]
    ppermute x12 -> x4, waiting for transfers between devices: 19.5 us -> 0.63 us  [swap(): lax.ppermute(value, axis, [(i, i ^ mask) for i in range(lax.axis_size(axi...]
    ppermute x0 -> x8, starting transfers between devices: none -> 17.7 us  [route(): return lax.ppermute(value, ('tile', 'col'), pairs)]
    ppermute x12 -> x4, starting transfers between devices: 15.6 us -> 10.6 us  [swap(): lax.ppermute(value, axis, [(i, i ^ mask) for i in range(lax.axis_size(axi...]
    unnamed x31 -> x30, local copies, waits for them, and re-layouts: 4.52 us -> 1.05 us
    pallas_call x1, Pallas kernels: 7.61 us -> 4.21 us  [pair_bias(): pl.pallas_call(functools.partial(bias_kernel, heads), grid=(rows // block...]
    ppermute x0 -> x8, waiting for transfers between devices: none -> 2.36 us  [route(): return lax.ppermute(value, ('tile', 'col'), pairs)]
    select_n x2 -> x0, other arithmetic: 1.85 us -> none  [the longest x1 0.92 us: exchanged(): gone = jnp.where(stays, other, tile_bias)]
  transfers between devices with their start and end apart: 12 -> 12, of which waited for: 4 -> 2; matrix products, arithmetic and copies ran while one was open for 4% -> 0% of each run, Pallas kernels for 29% -> 28%
where the time goes in v2:
time: 77.3 us; the launch traced here: 77 us
  Pallas kernels  44 us (57%)
  starting transfers between devices  28.2 us (36%)
  waiting for transfers between devices  2.99 us (4%)
  local copies, waits for them, and re-layouts  1.05 us (1%)
  between operations  0.8 us (1%)
    pallas_call x1, Pallas kernels, attention(): pl.pallas_call(functools.partial(attention_kernel, heads, cols), grid=(st...  17.7 us
    ppermute x8, starting transfers between devices, route(): return lax.ppermute(value, ('tile', 'col'), pairs)  17.7 us
    pallas_call x1, Pallas kernels, pair_update(): pl.pallas_call(functools.partial(pair_kernel, masks, upper, rows, extent)...  17.6 us
    ppermute x4, starting transfers between devices, swap(): lax.ppermute(value, axis, [(i, i ^ mask) for i in range(lax.axis_size(axi...  10.6 us
    pallas_call x1, Pallas kernels, factors(): pl.pallas_call(functools.partial(factors_kernel, rows, upper), grid=(rows...  4.5 us
    pallas_call x1, Pallas kernels, pair_bias(): pl.pallas_call(functools.partial(bias_kernel, heads), grid=(rows // block...  4.21 us
    ppermute x8, waiting for transfers between devices, route(): return lax.ppermute(value, ('tile', 'col'), pairs)  2.36 us
  transfers between devices with their start and end apart: 12, of which 2 were waited for; matrix products, arithmetic and copies ran while one was open for 0% of the time, Pallas kernels for 28%

profile of v2, /device:TPU:0, one launch (start us, length us, event | category | flops | bytes accessed | tf_op | source)
XLA Modules:
  0.0 77.0 jit_solution(6546073062349939345)
XLA Ops:
  0.6 4.5 %factors.1 = (bf16[16,128,256]{2,1,0:T(8,128)(2,1)}, bf16[256,128]{1,0:T(8,128)(2,1)}, bf16[256,128]{1,0:T(8,128)(2,1)}, bf16[512,128]{1,0:T(8,128)(2,1)}) custom-call(f32[16,128,256]{2,1,0:T(8,128)} %bitcast.15, f32[1,256]{1,0:T(1,128)} %bitcast.24, f32[1,256]{1,0:T(1,128)} %bitcast.25, bf16[32,256]{1,0:T(8,128)(2,1)} %bitcast.21, bf16[32,256]{1,0:T(8,128)(2,1)} %bitcast.22), custom_call_target="tpu_custom_call" | custom-call | flops 167772160 | bytes 3145728 | tf_op jit(solution)/shard_map/factors/pallas_call | solution.py:215
  5.1 0.0 copy-start.11
  5.2 0.0 copy-start
  5.2 4.1 %collective-permute-start.1 = (bf16[512,128]{1,0:T(8,128)(2,1)}, bf16[512,128]{1,0:T(8,128)(2,1)S(1)}, u32[]{:S(2)}, u32[]{:S(2)}) collective-permute-start(bf16[512,128]{1,0:T(8,128)(2,1)} %get-tuple-element.10.refs_4_), channel_id=1, source_target_pairs={{0,8},{4,12},{8,0},{12,4},{1,9},{5,13},{9,1},{13,5},{2,10},{6,14},... | collective-permute-start | bytes 393224 | tf_op jit(solution)/shard_map/ppermute | solution.py:619
  9.3 1.6 %collective-permute-start.10 = (bf16[512,128]{1,0:T(8,128)(2,1)}, bf16[512,128]{1,0:T(8,128)(2,1)S(1)}, u32[]{:S(2)}, u32[]{:S(2)}) collective-permute-start(bf16[512,128]{1,0:T(8,128)(2,1)} %get-tuple-element.10.refs_4_), channel_id=1, source_target_pairs={{0,4},{4,0},{8,12},{12,8},{1,5},{5,1},{9,13},{13,9},{2,6},{6,2},{1... | collective-permute-start | bytes 393224 | tf_op jit(solution)/shard_map/ppermute | solution.py:619
  10.9 1.5 %collective-permute-start.8 = (bf16[256,128]{1,0:T(8,128)(2,1)}, bf16[256,128]{1,0:T(8,128)(2,1)S(1)}, u32[]{:S(2)}, u32[]{:S(2)}) collective-permute-start(bf16[256,128]{1,0:T(8,128)(2,1)} %get-tuple-element.13), channel_id=1, source_target_pairs={{0,2},{2,10},{4,6},{6,14},{8,0},{10,8},{12,4},{14,12},{1,3},{3,11}... | collective-permute-start | bytes 196616 | tf_op jit(solution)/shard_map/ppermute | solution.py:635
  12.4 4.2 %pair_bias.1 = bf16[512,128]{1,0:T(8,128)(2,1)} custom-call(f32[64,128,128]{2,1,0:T(8,128)} %bitcast.13, f32[1,128]{1,0:T(1,128)} %bitcast.26, f32[8,128]{1,0:T(8,128)} %bitcast.23), custom_call_target="tpu_custom_call" | custom-call | flops 134217728 | bytes 4194304 | tf_op jit(solution)/shard_map/pair_bias/pallas_call | solution.py:264
  16.6 0.6 collective-permute-done.1.refs_5_
  17.2 0.0 collective-permute-start.11
  17.2 0.0 copy-done.14
  17.2 0.7 collective-permute-start.6
  17.9 0.0 copy-done.11
  17.9 5.0 %collective-permute-start.9 = (bf16[256,128]{1,0:T(8,128)(2,1)S(1)}, bf16[256,128]{1,0:T(8,128)(2,1)S(1)}, u32[]{:S(2)}, u32[]{:S(2)}) collective-permute-start(bf16[256,128]{1,0:T(8,128)(2,1)S(1)} %copy-done.11), channel_id=1, source_target_pairs={{0,6},{2,14},{4,2},{6,10},{8,4},{10,12},{12,0},{14,8},{1,7},{3,15}... | collective-permute-start | bytes 196616 | tf_op jit(solution)/shard_map/ppermute | solution.py:635
  22.9 0.0 collective-permute-done.8.refs_2_
  22.9 1.9 %collective-permute-start.7 = (bf16[256,128]{1,0:T(8,128)(2,1)S(1)}, bf16[256,128]{1,0:T(8,128)(2,1)S(1)}, u32[]{:S(2)}, u32[]{:S(2)}) collective-permute-start(bf16[256,128]{1,0:T(8,128)(2,1)S(1)} %copy-done.11), channel_id=1, source_target_pairs={{0,4},{2,12},{4,0},{6,8},{8,6},{10,14},{12,2},{14,10},{1,5},{3,13}... | collective-permute-start | bytes 196616 | tf_op jit(solution)/shard_map/ppermute | solution.py:635
  24.8 0.0 collective-permute-done.6.refs_0_
  24.8 0.0 copy-done
  24.8 4.8 %collective-permute-start = (bf16[16,128,256]{2,1,0:T(8,128)(2,1)S(1)}, bf16[16,128,256]{2,1,0:T(8,128)(2,1)S(1)}, u32[]{:S(2)}, u32[]{:S(2)}) collective-permute-start(bf16[16,128,256]{2,1,0:T(8,128)(2,1)S(1)} %copy-done), channel_id=1, source_target_pairs={{0,2},{2,0},{1,3},{3,1},{4,6},{6,4},{5,7},{7,5},{8,10},{10,8},{9,1... | collective-permute-start | bytes 3145736 | tf_op jit(solution)/shard_map/ppermute | solution.py:619
  29.7 0.0 collective-permute-done.9.refs_3_
  29.7 4.9 %collective-permute-start.5 = (bf16[8,64,128]{2,1,0:T(8,128)(2,1)}, bf16[8,64,128]{2,1,0:T(8,128)(2,1)S(1)}, u32[]{:S(2)}, u32[]{:S(2)}) collective-permute-start(bf16[8,64,128]{2,1,0:T(8,128)(2,1)} %bitcast.17), channel_id=1, source_target_pairs={{0,12},{2,8},{4,4},{6,0},{8,14},{10,10},{12,6},{14,2},{1,13},{3,9}... | collective-permute-start | bytes 393224 | tf_op jit(solution)/shard_map/ppermute | solution.py:635
  34.6 0.0 collective-permute-done.7.refs_1_
  34.6 0.0 copy-start.13
  34.6 1.7 %collective-permute-start.4 = (bf16[8,64,128]{2,1,0:T(8,128)(2,1)}, bf16[8,64,128]{2,1,0:T(8,128)(2,1)S(1)}, u32[]{:S(2)}, u32[]{:S(2)}) collective-permute-start(bf16[8,64,128]{2,1,0:T(8,128)(2,1)} %bitcast.18), channel_id=1, source_target_pairs={{0,8},{2,12},{4,0},{6,4},{8,10},{10,14},{12,2},{14,6},{1,9},{3,13}... | collective-permute-start | bytes 393224 | tf_op jit(solution)/shard_map/ppermute | solution.py:635
  36.4 0.0 collective-permute-done.10.refs_6_
  36.4 0.4 collective-permute-start.3
  36.7 0.0 collective-permute-done.11.refs_7_
  36.7 1.6 %collective-permute-start.2 = (bf16[8,64,128]{2,1,0:T(8,128)(2,1)}, bf16[8,64,128]{2,1,0:T(8,128)(2,1)S(1)}, u32[]{:S(2)}, u32[]{:S(2)}) collective-permute-start(bf16[8,64,128]{2,1,0:T(8,128)(2,1)} %bitcast.20), channel_id=1, source_target_pairs={{0,0},{2,4},{4,8},{6,12},{8,2},{10,6},{12,10},{14,14},{1,1},{3,5},... | collective-permute-start | bytes 393224 | tf_op jit(solution)/shard_map/ppermute | solution.py:635
  38.3 0.0 copy-done.2
  38.3 0.0 copy-done.9
  38.3 0.0 copy-done.10
  38.3 0.0 copy-done.12
  38.3 0.0 copy-done.13
  38.3 0.0 copy-done.3
  38.3 0.0 copy-done.4
  38.3 17.6 %pair_update.1 = f32[64,128,128]{2,1,0:T(8,128)} custom-call(bf16[256,128]{1,0:T(8,128)(2,1)} %copy-done.10, bf16[256,128]{1,0:T(8,128)(2,1)} %copy-done.13, bf16[256,128]{1,0:T(8,128)(2,1)} %copy-done.9, bf16[256,128]{1,0:T(8,128)(2,1)} %copy-done.12, bf16[512,128]{1,0:T(8,128)(2,1)} %get-tuple-element.10.refs_4_, bf16[512,128]{1,0:T(8,128)(2,1)} %copy-done.2, ...), custom_call_target="tpu_custom_call" | custom-call | flops 10737418240 | bytes 8388608 | tf_op jit(solution)/shard_map/pair_update/pallas_call | solution.py:392
  55.9 0.0 collective-permute-done.5.b3
  55.9 0.0 copy-start.5
  55.9 0.0 collective-permute-done.4.b2
  55.9 0.0 copy-start.6
  55.9 2.3 %collective-permute-done.3.b1 = bf16[8,64,128]{2,1,0:T(8,128)(2,1)S(1)} collective-permute-done((bf16[8,64,128]{2,1,0:T(8,128)(2,1)}, bf16[8,64,128]{2,1,0:T(8,128)(2,1)S(1)}, u32[]{:S(2)}, u32[]{:S(2)}) %collective-permute-start.3) | collective-permute-done | bytes 131104 | tf_op jit(solution)/shard_map/ppermute | solution.py:635
  58.3 0.0 collective-permute-done.2.b0
  58.3 0.0 collective-permute-done.far_ref
  58.3 0.0 copy-start.1
  58.3 0.0 copy-done.5
  58.3 0.6 copy-done.7
  58.9 0.1 copy-done.8
  59.0 0.3 copy-done.1
  59.3 17.7 %attention.1 = f32[16,128,256]{2,1,0:T(8,128)} custom-call(f32[16,128,256]{2,1,0:T(8,128)} %bitcast.16, bf16[16,128,256]{2,1,0:T(8,128)(2,1)} %get-tuple-element.9.own_ref, bf16[16,128,256]{2,1,0:T(8,128)(2,1)} %copy-done.1, bf16[8,64,128]{2,1,0:T(8,128)(2,1)} %copy-done.8, bf16[8,64,128]{2,1,0:T(8,128)(2,1)} %copy-done.7, bf16[8,64,128]{2,1,0:T(8,128)(2,1)} %copy-done.6, ...), custom_call_target="tpu_custom_call" | custom-call | flops 8053063680 | bytes 6291456 | tf_op jit(solution)/shard_map/attention/pallas_call | solution.py:557
  (10 shorter events, 0.0 us)
Async XLA Ops:
  5.1 12.1 %copy-start.14 = (bf16[256,128]{1,0:T(8,128)(2,1)S(1)}, bf16[256,128]{1,0:T(8,128)(2,1)}, u32[]{:S(2)}) copy-start(bf16[256,128]{1,0:T(8,128)(2,1)} %get-tuple-element.13) | copy-start | bytes 196612
  5.1 12.7 %copy-start.11 = (bf16[256,128]{1,0:T(8,128)(2,1)S(1)}, bf16[256,128]{1,0:T(8,128)(2,1)}, u32[]{:S(2)}) copy-start(bf16[256,128]{1,0:T(8,128)(2,1)} %get-tuple-element.14) | copy-start | bytes 196612
  5.2 19.7 %copy-start = (bf16[16,128,256]{2,1,0:T(8,128)(2,1)S(1)}, bf16[16,128,256]{2,1,0:T(8,128)(2,1)}, u32[]{:S(2)}) copy-start(bf16[16,128,256]{2,1,0:T(8,128)(2,1)} %get-tuple-element.9.own_ref) | copy-start | bytes 3145732
  5.2 12.0 %collective-permute-start.1 = (bf16[512,128]{1,0:T(8,128)(2,1)}, bf16[512,128]{1,0:T(8,128)(2,1)S(1)}, u32[]{:S(2)}, u32[]{:S(2)}) collective-permute-start(bf16[512,128]{1,0:T(8,128)(2,1)} %get-tuple-element.10.refs_4_), channel_id=1, source_target_pairs={{0,8},{4,12},{8,0},{12,4},{1,9},{5,13},{9,1},{13,5},{2,10},{6,14},... | collective-permute-start | bytes 393224 | tf_op jit(solution)/shard_map/ppermute | solution.py:619
  9.3 27.1 %collective-permute-start.10 = (bf16[512,128]{1,0:T(8,128)(2,1)}, bf16[512,128]{1,0:T(8,128)(2,1)S(1)}, u32[]{:S(2)}, u32[]{:S(2)}) collective-permute-start(bf16[512,128]{1,0:T(8,128)(2,1)} %get-tuple-element.10.refs_4_), channel_id=1, source_target_pairs={{0,4},{4,0},{8,12},{12,8},{1,5},{5,1},{9,13},{13,9},{2,6},{6,2},{1... | collective-permute-start | bytes 393224 | tf_op jit(solution)/shard_map/ppermute | solution.py:619
  10.9 12.0 %collective-permute-start.8 = (bf16[256,128]{1,0:T(8,128)(2,1)}, bf16[256,128]{1,0:T(8,128)(2,1)S(1)}, u32[]{:S(2)}, u32[]{:S(2)}) collective-permute-start(bf16[256,128]{1,0:T(8,128)(2,1)} %get-tuple-element.13), channel_id=1, source_target_pairs={{0,2},{2,10},{4,6},{6,14},{8,0},{10,8},{12,4},{14,12},{1,3},{3,11}... | collective-permute-start | bytes 196616 | tf_op jit(solution)/shard_map/ppermute | solution.py:635
  17.2 21.1 %copy-start.2 = (bf16[512,128]{1,0:T(8,128)(2,1)}, bf16[512,128]{1,0:T(8,128)(2,1)S(1)}, u32[]{:S(2)}) copy-start(bf16[512,128]{1,0:T(8,128)(2,1)S(1)} %collective-permute-done.1.refs_5_) | copy-start | bytes 393220
  17.2 19.5 %collective-permute-start.11 = (bf16[512,128]{1,0:T(8,128)(2,1)S(1)}, bf16[512,128]{1,0:T(8,128)(2,1)S(1)}, u32[]{:S(2)}, u32[]{:S(2)}) collective-permute-start(bf16[512,128]{1,0:T(8,128)(2,1)S(1)} %collective-permute-done.1.refs_5_), channel_id=1, source_target_pairs={{0,4},{4,0},{8,12},{12,8},{1,5},{5,1},{9,13},{13,9},{2,6},{6,2},{1... | collective-permute-start | bytes 393224 | tf_op jit(solution)/shard_map/ppermute | solution.py:619
  17.2 7.6 %collective-permute-start.6 = (bf16[256,128]{1,0:T(8,128)(2,1)S(1)}, bf16[256,128]{1,0:T(8,128)(2,1)S(1)}, u32[]{:S(2)}, u32[]{:S(2)}) collective-permute-start(bf16[256,128]{1,0:T(8,128)(2,1)S(1)} %copy-done.14), channel_id=1, source_target_pairs={{0,0},{2,8},{4,4},{6,12},{8,2},{10,10},{12,6},{14,14},{1,1},{3,9},... | collective-permute-start | bytes 196616 | tf_op jit(solution)/shard_map/ppermute | solution.py:635
  17.9 11.8 %collective-permute-start.9 = (bf16[256,128]{1,0:T(8,128)(2,1)S(1)}, bf16[256,128]{1,0:T(8,128)(2,1)S(1)}, u32[]{:S(2)}, u32[]{:S(2)}) collective-permute-start(bf16[256,128]{1,0:T(8,128)(2,1)S(1)} %copy-done.11), channel_id=1, source_target_pairs={{0,6},{2,14},{4,2},{6,10},{8,4},{10,12},{12,0},{14,8},{1,7},{3,15}... | collective-permute-start | bytes 196616 | tf_op jit(solution)/shard_map/ppermute | solution.py:635
  22.9 15.4 %copy-start.9 = (bf16[256,128]{1,0:T(8,128)(2,1)}, bf16[256,128]{1,0:T(8,128)(2,1)S(1)}, u32[]{:S(2)}) copy-start(bf16[256,128]{1,0:T(8,128)(2,1)S(1)} %collective-permute-done.8.refs_2_) | copy-start | bytes 196612
  22.9 11.7 %collective-permute-start.7 = (bf16[256,128]{1,0:T(8,128)(2,1)S(1)}, bf16[256,128]{1,0:T(8,128)(2,1)S(1)}, u32[]{:S(2)}, u32[]{:S(2)}) collective-permute-start(bf16[256,128]{1,0:T(8,128)(2,1)S(1)} %copy-done.11), channel_id=1, source_target_pairs={{0,4},{2,12},{4,0},{6,8},{8,6},{10,14},{12,2},{14,10},{1,5},{3,13}... | collective-permute-start | bytes 196616 | tf_op jit(solution)/shard_map/ppermute | solution.py:635
  24.8 13.5 %copy-start.10 = (bf16[256,128]{1,0:T(8,128)(2,1)}, bf16[256,128]{1,0:T(8,128)(2,1)S(1)}, u32[]{:S(2)}) copy-start(bf16[256,128]{1,0:T(8,128)(2,1)S(1)} %collective-permute-done.6.refs_0_) | copy-start | bytes 196612
  24.8 33.5 %collective-permute-start = (bf16[16,128,256]{2,1,0:T(8,128)(2,1)S(1)}, bf16[16,128,256]{2,1,0:T(8,128)(2,1)S(1)}, u32[]{:S(2)}, u32[]{:S(2)}) collective-permute-start(bf16[16,128,256]{2,1,0:T(8,128)(2,1)S(1)} %copy-done), channel_id=1, source_target_pairs={{0,2},{2,0},{1,3},{3,1},{4,6},{6,4},{5,7},{7,5},{8,10},{10,8},{9,1... | collective-permute-start | bytes 3145736 | tf_op jit(solution)/shard_map/ppermute | solution.py:619
  29.7 8.6 %copy-start.12 = (bf16[256,128]{1,0:T(8,128)(2,1)}, bf16[256,128]{1,0:T(8,128)(2,1)S(1)}, u32[]{:S(2)}) copy-start(bf16[256,128]{1,0:T(8,128)(2,1)S(1)} %collective-permute-done.9.refs_3_) | copy-start | bytes 196612
  29.7 26.2 %collective-permute-start.5 = (bf16[8,64,128]{2,1,0:T(8,128)(2,1)}, bf16[8,64,128]{2,1,0:T(8,128)(2,1)S(1)}, u32[]{:S(2)}, u32[]{:S(2)}) collective-permute-start(bf16[8,64,128]{2,1,0:T(8,128)(2,1)} %bitcast.17), channel_id=1, source_target_pairs={{0,12},{2,8},{4,4},{6,0},{8,14},{10,10},{12,6},{14,2},{1,13},{3,9}... | collective-permute-start | bytes 393224 | tf_op jit(solution)/shard_map/ppermute | solution.py:635
  34.6 3.7 %copy-start.13 = (bf16[256,128]{1,0:T(8,128)(2,1)}, bf16[256,128]{1,0:T(8,128)(2,1)S(1)}, u32[]{:S(2)}) copy-start(bf16[256,128]{1,0:T(8,128)(2,1)S(1)} %collective-permute-done.7.refs_1_) | copy-start | bytes 196612
  34.6 21.3 %collective-permute-start.4 = (bf16[8,64,128]{2,1,0:T(8,128)(2,1)}, bf16[8,64,128]{2,1,0:T(8,128)(2,1)S(1)}, u32[]{:S(2)}, u32[]{:S(2)}) collective-permute-start(bf16[8,64,128]{2,1,0:T(8,128)(2,1)} %bitcast.18), channel_id=1, source_target_pairs={{0,8},{2,12},{4,0},{6,4},{8,10},{10,14},{12,2},{14,6},{1,9},{3,13}... | collective-permute-start | bytes 393224 | tf_op jit(solution)/shard_map/ppermute | solution.py:635
  36.4 2.0 %copy-start.3 = (bf16[512,128]{1,0:T(8,128)(2,1)}, bf16[512,128]{1,0:T(8,128)(2,1)S(1)}, u32[]{:S(2)}) copy-start(bf16[512,128]{1,0:T(8,128)(2,1)S(1)} %collective-permute-done.10.refs_6_) | copy-start | bytes 393220
  36.4 21.9 %collective-permute-start.3 = (bf16[8,64,128]{2,1,0:T(8,128)(2,1)}, bf16[8,64,128]{2,1,0:T(8,128)(2,1)S(1)}, u32[]{:S(2)}, u32[]{:S(2)}) collective-permute-start(bf16[8,64,128]{2,1,0:T(8,128)(2,1)} %bitcast.19), channel_id=1, source_target_pairs={{0,4},{2,0},{4,12},{6,8},{8,6},{10,2},{12,14},{14,10},{1,5},{3,1},... | collective-permute-start | bytes 393224 | tf_op jit(solution)/shard_map/ppermute | solution.py:635
  36.7 1.6 %copy-start.4 = (bf16[512,128]{1,0:T(8,128)(2,1)}, bf16[512,128]{1,0:T(8,128)(2,1)S(1)}, u32[]{:S(2)}) copy-start(bf16[512,128]{1,0:T(8,128)(2,1)S(1)} %collective-permute-done.11.refs_7_) | copy-start | bytes 393220
  36.7 21.6 %collective-permute-start.2 = (bf16[8,64,128]{2,1,0:T(8,128)(2,1)}, bf16[8,64,128]{2,1,0:T(8,128)(2,1)S(1)}, u32[]{:S(2)}, u32[]{:S(2)}) collective-permute-start(bf16[8,64,128]{2,1,0:T(8,128)(2,1)} %bitcast.20), channel_id=1, source_target_pairs={{0,0},{2,4},{4,8},{6,12},{8,2},{10,6},{12,10},{14,14},{1,1},{3,5},... | collective-permute-start | bytes 393224 | tf_op jit(solution)/shard_map/ppermute | solution.py:635
  55.9 2.4 %copy-start.5 = (bf16[8,64,128]{2,1,0:T(8,128)(2,1)}, bf16[8,64,128]{2,1,0:T(8,128)(2,1)S(1)}, u32[]{:S(2)}) copy-start(bf16[8,64,128]{2,1,0:T(8,128)(2,1)S(1)} %collective-permute-done.5.b3) | copy-start | bytes 393220
  55.9 2.4 %copy-start.6 = (bf16[8,64,128]{2,1,0:T(8,128)(2,1)}, bf16[8,64,128]{2,1,0:T(8,128)(2,1)S(1)}, u32[]{:S(2)}) copy-start(bf16[8,64,128]{2,1,0:T(8,128)(2,1)S(1)} %collective-permute-done.4.b2) | copy-start | bytes 393220
  58.3 0.6 copy-start.7
  58.3 0.7 copy-start.8
  58.3 1.0 %copy-start.1 = (bf16[16,128,256]{2,1,0:T(8,128)(2,1)}, bf16[16,128,256]{2,1,0:T(8,128)(2,1)S(1)}, u32[]{:S(2)}) copy-start(bf16[16,128,256]{2,1,0:T(8,128)(2,1)S(1)} %collective-permute-done.far_ref) | copy-start | bytes 3145732

commit v3 on v2

--- a/solution.py
+++ b/solution.py
@@ -285,7 +285,7 @@
     parts = len(masks)
     lefts, rights = refs[:parts], refs[parts : 2 * parts]
     pair_ref, map_ref, gain_ref, wide_ref, shrink_ref, out_ref = refs[2 * parts : 2 * parts + 6]
-    rall, lall, outer, maps, wt, wide_t, shrink_t, gains, middle, normed, hidden = refs[2 * parts + 6 :]
+    rall, lall, outer_a, outer_b, maps, wt, wide_t, shrink_t, gains, middle, normed, hidden = refs[2 * parts + 6 :]
     step = pl.program_id(0)
     last = pl.num_programs(0) - 1
     block, cols, _ = pair_ref.shape
@@ -310,7 +310,6 @@
         shrink_t[...] = shrink_ref[...].T
         gains[...] = jnp.broadcast_to(down(gain_ref[...]), gains.shape)
 
-    fresh, ready = step % 2, (step + 1) % 2
     duo = 2
     size = block * extent
     first = pl.multiple_of(jnp.minimum(step, last - 1) * size, size)
@@ -318,7 +317,7 @@
     heights = 2 if block % 4 == 0 else 1
     height = block // heights
 
-    def product(n):
+    def product(outer, n):
         c, v = n // heights, n % heights
         lanes = slice(c * duo * cols, (c + 1) * duo * cols)
         start = pl.multiple_of(first + v * height * extent, height * extent)
@@ -327,12 +326,12 @@
             row = v * height + i
             for d in range(duo):
                 at = (c * duo + d) * extent
-                outer[fresh, row // 2, at : at + extent, row % 2 * cols : (row % 2 + 1) * cols] = made[
+                outer[row // 2, at : at + extent, row % 2 * cols : (row % 2 + 1) * cols] = made[
                     i * extent : (i + 1) * extent, d * cols : (d + 1) * cols
                 ]
 
-    def update(k):
-        mid = dot(wt[...], outer[ready, k])
+    def update(outer, k):
+        mid = dot(wt[...], outer[k])
         middle[k] = mid + jnp.concatenate([pair_ref[2 * k].T, pair_ref[2 * k + 1].T], axis=1)
 
     def scale(k):
@@ -350,36 +349,43 @@
             out_ref[2 * k + i] = done[:, i * cols : (i + 1) * cols].T
 
     pairs = block // 2
-    stages = (
-        (0, update),
-        (1, scale),
-        (2, functools.partial(widen, 0)),
-        (2, functools.partial(widen, 1)),
-        (3, shrink),
-    )
-    feed = []
-    for t in range(pairs + 3):
-        for lag, stage in stages:
-            if 0 <= t - lag < pairs:
-                feed.append(functools.partial(stage, t - lag))
+
+    def feed(outer):
+        stages = (
+            (0, functools.partial(update, outer)),
+            (1, scale),
+            (2, functools.partial(widen, 0)),
+            (2, functools.partial(widen, 1)),
+            (3, shrink),
+        )
+        pieces = []
+        for t in range(pairs + 3):
+            for lag, stage in stages:
+                if 0 <= t - lag < pairs:
+                    pieces.append(functools.partial(stage, t - lag))
+        return pieces
+
     chunks = extent // duo * heights
 
     @pl.when(step == 0)
     def _():
         for c in range(chunks):
-            product(c)
-
-    @pl.when((step > 0) & (step < last))
-    def _():
-        for n, piece in enumerate(feed):
-            for c in range(n * chunks // len(feed), (n + 1) * chunks // len(feed)):
-                product(c)
-            piece()
-
-    @pl.when(step == last)
-    def _():
-        for piece in feed:
-            piece()
+            product(outer_a, c)
+
+    for odd, (made, used) in enumerate(((outer_a, outer_b), (outer_b, outer_a))):
+
+        @pl.when((step > 0) & (step < last) & (step % 2 == odd))
+        def _(made=made, used=used):
+            pieces = feed(used)
+            for n, piece in enumerate(pieces):
+                for c in range(n * chunks // len(pieces), (n + 1) * chunks // len(pieces)):
+                    product(made, c)
+                piece()
+
+        @pl.when((step == last) & (step % 2 == odd))
+        def _(used=used):
+            for piece in feed(used):
+                piece()
 
 
 def pair_update(lefts, rights, masks, upper, pair, maps, gain, wide, shrink, rows, block):
@@ -399,7 +405,7 @@
         scratch_shapes=[
             pltpu.VMEM((parts * rows, extent * cols), jnp.bfloat16),
             pltpu.VMEM((tile_rows * extent, parts * rows), jnp.bfloat16),
-            pltpu.VMEM((2, pairs, extent * extent, 2 * cols), jnp.bfloat16),
+            *[pltpu.VMEM((pairs, extent * extent, 2 * cols), jnp.bfloat16)] * 2,
             pltpu.VMEM((extent * extent, channels), jnp.float32),
             pltpu.VMEM((channels, extent * extent), jnp.bfloat16),
             pltpu.VMEM(wide.shape[::-1], jnp.bfloat16),
@@ -479,7 +485,7 @@
         middle[...] = mid
         normed[...] = (normalized_down(mid) * gains[...]).astype(bf16)
 
-    widths = 16
+    widths = 4
     chunk = hidden.shape[0] // widths
     part = features // 2
 
@@ -521,8 +527,9 @@
                     attend(t - 2)
                 if t < units:
                     scores(t, i)
-                if left:
-                    left.pop(0)()
+                turns, turn = 2 * (units + 2), 2 * t + i
+                for piece in left[turn * len(left) // turns : (turn + 1) * len(left) // turns]:
+                    piece()
                 if 1 <= t <= units:
                     soften(t - 1, i)
 
@@ -670,7 +677,7 @@
         feedforward_scale,
         alignment_widen_map,
         alignment_shrink_map,
-        2,
+        4,
     )
     return (alignment_revised[None], grid_revised[None])
 

time: 77.3 us -> 76.3 us (0.987)
  Pallas kernels: 44 us -> 40.4 us
  waiting for transfers between devices: 2.99 us -> 5.57 us
    pallas_call x1, Pallas kernels: 17.6 us -> 15 us  [pair_update(): pl.pallas_call(functools.partial(pair_kernel, masks, upper, rows, extent)...]
    ppermute x8, waiting for transfers between devices: 2.36 us -> 4.94 us  [route(): return lax.ppermute(value, ('tile', 'col'), pairs)]
    pallas_call x1, Pallas kernels: 17.7 us -> 16.7 us  [attention(): pl.pallas_call(functools.partial(attention_kernel, heads, cols), grid=(st...]
  transfers between devices with their start and end apart: 12 -> 12, of which waited for: 2 -> 2; matrix products, arithmetic and copies ran while one was open for 0% -> 0% of each run, Pallas kernels for 28% -> 25%
where the time goes in v3:
time: 76.3 us; the launch traced here: 76 us
  Pallas kernels  40.4 us (53%)
  starting transfers between devices  28.2 us (37%)
  waiting for transfers between devices  5.57 us (7%)
  local copies, waits for them, and re-layouts  1.05 us (1%)
  between operations  0.8 us (1%)
    ppermute x8, starting transfers between devices, route(): return lax.ppermute(value, ('tile', 'col'), pairs)  17.7 us
    pallas_call x1, Pallas kernels, attention(): pl.pallas_call(functools.partial(attention_kernel, heads, cols), grid=(st...  16.7 us
    pallas_call x1, Pallas kernels, pair_update(): pl.pallas_call(functools.partial(pair_kernel, masks, upper, rows, extent)...  15 us
    ppermute x4, starting transfers between devices, swap(): lax.ppermute(value, axis, [(i, i ^ mask) for i in range(lax.axis_size(axi...  10.6 us
    ppermute x8, waiting for transfers between devices, route(): return lax.ppermute(value, ('tile', 'col'), pairs)  4.94 us
    pallas_call x1, Pallas kernels, factors(): pl.pallas_call(functools.partial(factors_kernel, rows, upper), grid=(rows...  4.5 us
    pallas_call x1, Pallas kernels, pair_bias(): pl.pallas_call(functools.partial(bias_kernel, heads), grid=(rows // block...  4.21 us
  transfers between devices with their start and end apart: 12, of which 2 were waited for; matrix products, arithmetic and copies ran while one was open for 0% of the time, Pallas kernels for 25%

profile of v3, /device:TPU:0, one launch (start us, length us, event | category | flops | bytes accessed | tf_op | source)
XLA Modules:
  0.0 76.0 jit_solution(11546613150189783125)
XLA Ops:
  0.6 4.5 %factors.1 = (bf16[16,128,256]{2,1,0:T(8,128)(2,1)}, bf16[256,128]{1,0:T(8,128)(2,1)}, bf16[256,128]{1,0:T(8,128)(2,1)}, bf16[512,128]{1,0:T(8,128)(2,1)}) custom-call(f32[16,128,256]{2,1,0:T(8,128)} %bitcast.15, f32[1,256]{1,0:T(1,128)} %bitcast.24, f32[1,256]{1,0:T(1,128)} %bitcast.25, bf16[32,256]{1,0:T(8,128)(2,1)} %bitcast.21, bf16[32,256]{1,0:T(8,128)(2,1)} %bitcast.22), custom_call_target="tpu_custom_call" | custom-call | flops 167772160 | bytes 3145728 | tf_op jit(solution)/shard_map/factors/pallas_call | solution.py:215
  5.1 0.0 copy-start.11
  5.2 0.0 copy-start
  5.2 4.1 %collective-permute-start.1 = (bf16[512,128]{1,0:T(8,128)(2,1)}, bf16[512,128]{1,0:T(8,128)(2,1)S(1)}, u32[]{:S(2)}, u32[]{:S(2)}) collective-permute-start(bf16[512,128]{1,0:T(8,128)(2,1)} %get-tuple-element.10.refs_4_), channel_id=1, source_target_pairs={{0,8},{4,12},{8,0},{12,4},{1,9},{5,13},{9,1},{13,5},{2,10},{6,14},... | collective-permute-start | bytes 393224 | tf_op jit(solution)/shard_map/ppermute | solution.py:626
  9.3 1.6 %collective-permute-start.10 = (bf16[512,128]{1,0:T(8,128)(2,1)}, bf16[512,128]{1,0:T(8,128)(2,1)S(1)}, u32[]{:S(2)}, u32[]{:S(2)}) collective-permute-start(bf16[512,128]{1,0:T(8,128)(2,1)} %get-tuple-element.10.refs_4_), channel_id=1, source_target_pairs={{0,4},{4,0},{8,12},{12,8},{1,5},{5,1},{9,13},{13,9},{2,6},{6,2},{1... | collective-permute-start | bytes 393224 | tf_op jit(solution)/shard_map/ppermute | solution.py:626
  10.9 1.5 %collective-permute-start.8 = (bf16[256,128]{1,0:T(8,128)(2,1)}, bf16[256,128]{1,0:T(8,128)(2,1)S(1)}, u32[]{:S(2)}, u32[]{:S(2)}) collective-permute-start(bf16[256,128]{1,0:T(8,128)(2,1)} %get-tuple-element.13), channel_id=1, source_target_pairs={{0,2},{2,10},{4,6},{6,14},{8,0},{10,8},{12,4},{14,12},{1,3},{3,11}... | collective-permute-start | bytes 196616 | tf_op jit(solution)/shard_map/ppermute | solution.py:642
  12.4 4.2 %pair_bias.1 = bf16[512,128]{1,0:T(8,128)(2,1)} custom-call(f32[64,128,128]{2,1,0:T(8,128)} %bitcast.13, f32[1,128]{1,0:T(1,128)} %bitcast.26, f32[8,128]{1,0:T(8,128)} %bitcast.23), custom_call_target="tpu_custom_call" | custom-call | flops 134217728 | bytes 4194304 | tf_op jit(solution)/shard_map/pair_bias/pallas_call | solution.py:264
  16.6 0.6 collective-permute-done.1.refs_5_
  17.2 0.0 collective-permute-start.11
  17.2 0.0 copy-done.14
  17.2 0.7 collective-permute-start.6
  17.9 0.0 copy-done.11
  17.9 5.0 %collective-permute-start.9 = (bf16[256,128]{1,0:T(8,128)(2,1)S(1)}, bf16[256,128]{1,0:T(8,128)(2,1)S(1)}, u32[]{:S(2)}, u32[]{:S(2)}) collective-permute-start(bf16[256,128]{1,0:T(8,128)(2,1)S(1)} %copy-done.11), channel_id=1, source_target_pairs={{0,6},{2,14},{4,2},{6,10},{8,4},{10,12},{12,0},{14,8},{1,7},{3,15}... | collective-permute-start | bytes 196616 | tf_op jit(solution)/shard_map/ppermute | solution.py:642
  22.9 0.0 collective-permute-done.8.refs_2_
  22.9 1.9 %collective-permute-start.7 = (bf16[256,128]{1,0:T(8,128)(2,1)S(1)}, bf16[256,128]{1,0:T(8,128)(2,1)S(1)}, u32[]{:S(2)}, u32[]{:S(2)}) collective-permute-start(bf16[256,128]{1,0:T(8,128)(2,1)S(1)} %copy-done.11), channel_id=1, source_target_pairs={{0,4},{2,12},{4,0},{6,8},{8,6},{10,14},{12,2},{14,10},{1,5},{3,13}... | collective-permute-start | bytes 196616 | tf_op jit(solution)/shard_map/ppermute | solution.py:642
  24.8 0.0 collective-permute-done.6.refs_0_
  24.8 0.0 copy-done
  24.8 4.8 %collective-permute-start = (bf16[16,128,256]{2,1,0:T(8,128)(2,1)S(1)}, bf16[16,128,256]{2,1,0:T(8,128)(2,1)S(1)}, u32[]{:S(2)}, u32[]{:S(2)}) collective-permute-start(bf16[16,128,256]{2,1,0:T(8,128)(2,1)S(1)} %copy-done), channel_id=1, source_target_pairs={{0,2},{2,0},{1,3},{3,1},{4,6},{6,4},{5,7},{7,5},{8,10},{10,8},{9,1... | collective-permute-start | bytes 3145736 | tf_op jit(solution)/shard_map/ppermute | solution.py:626
  29.7 0.0 collective-permute-done.9.refs_3_
  29.7 4.9 %collective-permute-start.5 = (bf16[8,64,128]{2,1,0:T(8,128)(2,1)}, bf16[8,64,128]{2,1,0:T(8,128)(2,1)S(1)}, u32[]{:S(2)}, u32[]{:S(2)}) collective-permute-start(bf16[8,64,128]{2,1,0:T(8,128)(2,1)} %bitcast.17), channel_id=1, source_target_pairs={{0,12},{2,8},{4,4},{6,0},{8,14},{10,10},{12,6},{14,2},{1,13},{3,9}... | collective-permute-start | bytes 393224 | tf_op jit(solution)/shard_map/ppermute | solution.py:642
  34.6 0.0 collective-permute-done.7.refs_1_
  34.6 0.0 copy-start.13
  34.6 1.7 %collective-permute-start.4 = (bf16[8,64,128]{2,1,0:T(8,128)(2,1)}, bf16[8,64,128]{2,1,0:T(8,128)(2,1)S(1)}, u32[]{:S(2)}, u32[]{:S(2)}) collective-permute-start(bf16[8,64,128]{2,1,0:T(8,128)(2,1)} %bitcast.18), channel_id=1, source_target_pairs={{0,8},{2,12},{4,0},{6,4},{8,10},{10,14},{12,2},{14,6},{1,9},{3,13}... | collective-permute-start | bytes 393224 | tf_op jit(solution)/shard_map/ppermute | solution.py:642
  36.4 0.0 collective-permute-done.10.refs_6_
  36.4 0.4 collective-permute-start.3
  36.7 0.0 collective-permute-done.11.refs_7_
  36.7 1.6 %collective-permute-start.2 = (bf16[8,64,128]{2,1,0:T(8,128)(2,1)}, bf16[8,64,128]{2,1,0:T(8,128)(2,1)S(1)}, u32[]{:S(2)}, u32[]{:S(2)}) collective-permute-start(bf16[8,64,128]{2,1,0:T(8,128)(2,1)} %bitcast.20), channel_id=1, source_target_pairs={{0,0},{2,4},{4,8},{6,12},{8,2},{10,6},{12,10},{14,14},{1,1},{3,5},... | collective-permute-start | bytes 393224 | tf_op jit(solution)/shard_map/ppermute | solution.py:642
  38.3 0.0 copy-done.2
  38.3 0.0 copy-done.9
  38.3 0.0 copy-done.10
  38.3 0.0 copy-done.12
  38.3 0.0 copy-done.13
  38.3 0.0 copy-done.3
  38.3 0.0 copy-done.4
  38.3 15.0 %pair_update.1 = f32[64,128,128]{2,1,0:T(8,128)} custom-call(bf16[256,128]{1,0:T(8,128)(2,1)} %copy-done.10, bf16[256,128]{1,0:T(8,128)(2,1)} %copy-done.13, bf16[256,128]{1,0:T(8,128)(2,1)} %copy-done.9, bf16[256,128]{1,0:T(8,128)(2,1)} %copy-done.12, bf16[512,128]{1,0:T(8,128)(2,1)} %get-tuple-element.10.refs_4_, bf16[512,128]{1,0:T(8,128)(2,1)} %copy-done.2, ...), custom_call_target="tpu_custom_call" | custom-call | flops 10737418240 | bytes 8388608 | tf_op jit(solution)/shard_map/pair_update/pallas_call | solution.py:398
  53.3 0.0 collective-permute-done.5.b3
  53.3 0.0 copy-start.5
  53.3 0.0 collective-permute-done.4.b2
  53.4 0.0 copy-start.6
  53.4 4.9 %collective-permute-done.3.b1 = bf16[8,64,128]{2,1,0:T(8,128)(2,1)S(1)} collective-permute-done((bf16[8,64,128]{2,1,0:T(8,128)(2,1)}, bf16[8,64,128]{2,1,0:T(8,128)(2,1)S(1)}, u32[]{:S(2)}, u32[]{:S(2)}) %collective-permute-start.3) | collective-permute-done | bytes 131104 | tf_op jit(solution)/shard_map/ppermute | solution.py:642
  58.3 0.0 collective-permute-done.2.b0
  58.3 0.0 collective-permute-done.far_ref
  58.3 0.0 copy-start.1
  58.3 0.0 copy-done.5
  58.3 0.6 copy-done.7
  58.9 0.1 copy-done.8
  59.0 0.3 copy-done.1
  59.3 16.7 %attention.1 = f32[16,128,256]{2,1,0:T(8,128)} custom-call(f32[16,128,256]{2,1,0:T(8,128)} %bitcast.16, bf16[16,128,256]{2,1,0:T(8,128)(2,1)} %get-tuple-element.9.own_ref, bf16[16,128,256]{2,1,0:T(8,128)(2,1)} %copy-done.1, bf16[8,64,128]{2,1,0:T(8,128)(2,1)} %copy-done.8, bf16[8,64,128]{2,1,0:T(8,128)(2,1)} %copy-done.7, bf16[8,64,128]{2,1,0:T(8,128)(2,1)} %copy-done.6, ...), custom_call_target="tpu_custom_call" | custom-call | flops 8053063680 | bytes 6291456 | tf_op jit(solution)/shard_map/attention/pallas_call | solution.py:564
  (10 shorter events, 0.0 us)
Async XLA Ops:
  5.1 12.1 %copy-start.14 = (bf16[256,128]{1,0:T(8,128)(2,1)S(1)}, bf16[256,128]{1,0:T(8,128)(2,1)}, u32[]{:S(2)}) copy-start(bf16[256,128]{1,0:T(8,128)(2,1)} %get-tuple-element.13) | copy-start | bytes 196612
  5.1 12.7 %copy-start.11 = (bf16[256,128]{1,0:T(8,128)(2,1)S(1)}, bf16[256,128]{1,0:T(8,128)(2,1)}, u32[]{:S(2)}) copy-start(bf16[256,128]{1,0:T(8,128)(2,1)} %get-tuple-element.14) | copy-start | bytes 196612
  5.2 19.7 %copy-start = (bf16[16,128,256]{2,1,0:T(8,128)(2,1)S(1)}, bf16[16,128,256]{2,1,0:T(8,128)(2,1)}, u32[]{:S(2)}) copy-start(bf16[16,128,256]{2,1,0:T(8,128)(2,1)} %get-tuple-element.9.own_ref) | copy-start | bytes 3145732
  5.2 12.0 %collective-permute-start.1 = (bf16[512,128]{1,0:T(8,128)(2,1)}, bf16[512,128]{1,0:T(8,128)(2,1)S(1)}, u32[]{:S(2)}, u32[]{:S(2)}) collective-permute-start(bf16[512,128]{1,0:T(8,128)(2,1)} %get-tuple-element.10.refs_4_), channel_id=1, source_target_pairs={{0,8},{4,12},{8,0},{12,4},{1,9},{5,13},{9,1},{13,5},{2,10},{6,14},... | collective-permute-start | bytes 393224 | tf_op jit(solution)/shard_map/ppermute | solution.py:626
  9.3 27.1 %collective-permute-start.10 = (bf16[512,128]{1,0:T(8,128)(2,1)}, bf16[512,128]{1,0:T(8,128)(2,1)S(1)}, u32[]{:S(2)}, u32[]{:S(2)}) collective-permute-start(bf16[512,128]{1,0:T(8,128)(2,1)} %get-tuple-element.10.refs_4_), channel_id=1, source_target_pairs={{0,4},{4,0},{8,12},{12,8},{1,5},{5,1},{9,13},{13,9},{2,6},{6,2},{1... | collective-permute-start | bytes 393224 | tf_op jit(solution)/shard_map/ppermute | solution.py:626
  10.9 12.0 %collective-permute-start.8 = (bf16[256,128]{1,0:T(8,128)(2,1)}, bf16[256,128]{1,0:T(8,128)(2,1)S(1)}, u32[]{:S(2)}, u32[]{:S(2)}) collective-permute-start(bf16[256,128]{1,0:T(8,128)(2,1)} %get-tuple-element.13), channel_id=1, source_target_pairs={{0,2},{2,10},{4,6},{6,14},{8,0},{10,8},{12,4},{14,12},{1,3},{3,11}... | collective-permute-start | bytes 196616 | tf_op jit(solution)/shard_map/ppermute | solution.py:642
  17.2 21.1 %copy-start.2 = (bf16[512,128]{1,0:T(8,128)(2,1)}, bf16[512,128]{1,0:T(8,128)(2,1)S(1)}, u32[]{:S(2)}) copy-start(bf16[512,128]{1,0:T(8,128)(2,1)S(1)} %collective-permute-done.1.refs_5_) | copy-start | bytes 393220
  17.2 19.5 %collective-permute-start.11 = (bf16[512,128]{1,0:T(8,128)(2,1)S(1)}, bf16[512,128]{1,0:T(8,128)(2,1)S(1)}, u32[]{:S(2)}, u32[]{:S(2)}) collective-permute-start(bf16[512,128]{1,0:T(8,128)(2,1)S(1)} %collective-permute-done.1.refs_5_), channel_id=1, source_target_pairs={{0,4},{4,0},{8,12},{12,8},{1,5},{5,1},{9,13},{13,9},{2,6},{6,2},{1... | collective-permute-start | bytes 393224 | tf_op jit(solution)/shard_map/ppermute | solution.py:626
  17.2 7.6 %collective-permute-start.6 = (bf16[256,128]{1,0:T(8,128)(2,1)S(1)}, bf16[256,128]{1,0:T(8,128)(2,1)S(1)}, u32[]{:S(2)}, u32[]{:S(2)}) collective-permute-start(bf16[256,128]{1,0:T(8,128)(2,1)S(1)} %copy-done.14), channel_id=1, source_target_pairs={{0,0},{2,8},{4,4},{6,12},{8,2},{10,10},{12,6},{14,14},{1,1},{3,9},... | collective-permute-start | bytes 196616 | tf_op jit(solution)/shard_map/ppermute | solution.py:642
  17.9 11.8 %collective-permute-start.9 = (bf16[256,128]{1,0:T(8,128)(2,1)S(1)}, bf16[256,128]{1,0:T(8,128)(2,1)S(1)}, u32[]{:S(2)}, u32[]{:S(2)}) collective-permute-start(bf16[256,128]{1,0:T(8,128)(2,1)S(1)} %copy-done.11), channel_id=1, source_target_pairs={{0,6},{2,14},{4,2},{6,10},{8,4},{10,12},{12,0},{14,8},{1,7},{3,15}... | collective-permute-start | bytes 196616 | tf_op jit(solution)/shard_map/ppermute | solution.py:642
  22.9 15.4 %copy-start.9 = (bf16[256,128]{1,0:T(8,128)(2,1)}, bf16[256,128]{1,0:T(8,128)(2,1)S(1)}, u32[]{:S(2)}) copy-start(bf16[256,128]{1,0:T(8,128)(2,1)S(1)} %collective-permute-done.8.refs_2_) | copy-start | bytes 196612
  22.9 11.7 %collective-permute-start.7 = (bf16[256,128]{1,0:T(8,128)(2,1)S(1)}, bf16[256,128]{1,0:T(8,128)(2,1)S(1)}, u32[]{:S(2)}, u32[]{:S(2)}) collective-permute-start(bf16[256,128]{1,0:T(8,128)(2,1)S(1)} %copy-done.11), channel_id=1, source_target_pairs={{0,4},{2,12},{4,0},{6,8},{8,6},{10,14},{12,2},{14,10},{1,5},{3,13}... | collective-permute-start | bytes 196616 | tf_op jit(solution)/shard_map/ppermute | solution.py:642
  24.8 13.5 %copy-start.10 = (bf16[256,128]{1,0:T(8,128)(2,1)}, bf16[256,128]{1,0:T(8,128)(2,1)S(1)}, u32[]{:S(2)}) copy-start(bf16[256,128]{1,0:T(8,128)(2,1)S(1)} %collective-permute-done.6.refs_0_) | copy-start | bytes 196612
  24.8 33.5 %collective-permute-start = (bf16[16,128,256]{2,1,0:T(8,128)(2,1)S(1)}, bf16[16,128,256]{2,1,0:T(8,128)(2,1)S(1)}, u32[]{:S(2)}, u32[]{:S(2)}) collective-permute-start(bf16[16,128,256]{2,1,0:T(8,128)(2,1)S(1)} %copy-done), channel_id=1, source_target_pairs={{0,2},{2,0},{1,3},{3,1},{4,6},{6,4},{5,7},{7,5},{8,10},{10,8},{9,1... | collective-permute-start | bytes 3145736 | tf_op jit(solution)/shard_map/ppermute | solution.py:626
  29.7 8.6 %copy-start.12 = (bf16[256,128]{1,0:T(8,128)(2,1)}, bf16[256,128]{1,0:T(8,128)(2,1)S(1)}, u32[]{:S(2)}) copy-start(bf16[256,128]{1,0:T(8,128)(2,1)S(1)} %collective-permute-done.9.refs_3_) | copy-start | bytes 196612
  29.7 23.7 %collective-permute-start.5 = (bf16[8,64,128]{2,1,0:T(8,128)(2,1)}, bf16[8,64,128]{2,1,0:T(8,128)(2,1)S(1)}, u32[]{:S(2)}, u32[]{:S(2)}) collective-permute-start(bf16[8,64,128]{2,1,0:T(8,128)(2,1)} %bitcast.17), channel_id=1, source_target_pairs={{0,12},{2,8},{4,4},{6,0},{8,14},{10,10},{12,6},{14,2},{1,13},{3,9}... | collective-permute-start | bytes 393224 | tf_op jit(solution)/shard_map/ppermute | solution.py:642
  34.6 3.7 %copy-start.13 = (bf16[256,128]{1,0:T(8,128)(2,1)}, bf16[256,128]{1,0:T(8,128)(2,1)S(1)}, u32[]{:S(2)}) copy-start(bf16[256,128]{1,0:T(8,128)(2,1)S(1)} %collective-permute-done.7.refs_1_) | copy-start | bytes 196612
  34.6 18.7 %collective-permute-start.4 = (bf16[8,64,128]{2,1,0:T(8,128)(2,1)}, bf16[8,64,128]{2,1,0:T(8,128)(2,1)S(1)}, u32[]{:S(2)}, u32[]{:S(2)}) collective-permute-start(bf16[8,64,128]{2,1,0:T(8,128)(2,1)} %bitcast.18), channel_id=1, source_target_pairs={{0,8},{2,12},{4,0},{6,4},{8,10},{10,14},{12,2},{14,6},{1,9},{3,13}... | collective-permute-start | bytes 393224 | tf_op jit(solution)/shard_map/ppermute | solution.py:642
  36.4 2.0 %copy-start.3 = (bf16[512,128]{1,0:T(8,128)(2,1)}, bf16[512,128]{1,0:T(8,128)(2,1)S(1)}, u32[]{:S(2)}) copy-start(bf16[512,128]{1,0:T(8,128)(2,1)S(1)} %collective-permute-done.10.refs_6_) | copy-start | bytes 393220
  36.4 21.9 %collective-permute-start.3 = (bf16[8,64,128]{2,1,0:T(8,128)(2,1)}, bf16[8,64,128]{2,1,0:T(8,128)(2,1)S(1)}, u32[]{:S(2)}, u32[]{:S(2)}) collective-permute-start(bf16[8,64,128]{2,1,0:T(8,128)(2,1)} %bitcast.19), channel_id=1, source_target_pairs={{0,4},{2,0},{4,12},{6,8},{8,6},{10,2},{12,14},{14,10},{1,5},{3,1},... | collective-permute-start | bytes 393224 | tf_op jit(solution)/shard_map/ppermute | solution.py:642
  36.7 1.6 %copy-start.4 = (bf16[512,128]{1,0:T(8,128)(2,1)}, bf16[512,128]{1,0:T(8,128)(2,1)S(1)}, u32[]{:S(2)}) copy-start(bf16[512,128]{1,0:T(8,128)(2,1)S(1)} %collective-permute-done.11.refs_7_) | copy-start | bytes 393220
  36.7 21.6 %collective-permute-start.2 = (bf16[8,64,128]{2,1,0:T(8,128)(2,1)}, bf16[8,64,128]{2,1,0:T(8,128)(2,1)S(1)}, u32[]{:S(2)}, u32[]{:S(2)}) collective-permute-start(bf16[8,64,128]{2,1,0:T(8,128)(2,1)} %bitcast.20), channel_id=1, source_target_pairs={{0,0},{2,4},{4,8},{6,12},{8,2},{10,6},{12,10},{14,14},{1,1},{3,5},... | collective-permute-start | bytes 393224 | tf_op jit(solution)/shard_map/ppermute | solution.py:642
  53.3 5.0 %copy-start.5 = (bf16[8,64,128]{2,1,0:T(8,128)(2,1)}, bf16[8,64,128]{2,1,0:T(8,128)(2,1)S(1)}, u32[]{:S(2)}) copy-start(bf16[8,64,128]{2,1,0:T(8,128)(2,1)S(1)} %collective-permute-done.5.b3) | copy-start | bytes 393220
  53.4 5.0 %copy-start.6 = (bf16[8,64,128]{2,1,0:T(8,128)(2,1)}, bf16[8,64,128]{2,1,0:T(8,128)(2,1)S(1)}, u32[]{:S(2)}) copy-start(bf16[8,64,128]{2,1,0:T(8,128)(2,1)S(1)} %collective-permute-done.4.b2) | copy-start | bytes 393220
  58.3 0.6 copy-start.7
  58.3 0.7 copy-start.8
  58.3 1.0 %copy-start.1 = (bf16[16,128,256]{2,1,0:T(8,128)(2,1)}, bf16[16,128,256]{2,1,0:T(8,128)(2,1)S(1)}, u32[]{:S(2)}) copy-start(bf16[16,128,256]{2,1,0:T(8,128)(2,1)S(1)} %collective-permute-done.far_ref) | copy-start | bytes 3145732
